TPU v7x, 256 devices: a whole 4x4x8 slice. The times are simulated.
256 devices in a mesh: view: 16 (over x, z_hi), tile: 16 (over y, z_lo, core).
Axes of the slice: x: 4, y: 4, z: 8 (z_hi: 4, z_lo: 2; z = z_hi * 2 + z_lo), core: 2. Of those that a mesh axis runs over, the one named last changes fastest.
Arguments:
- ref_feat: bfloat16 [32, 32768], P(None, 'tile'), may hold values from -6 to 6
- src_feat: bfloat16 [16, 16, 32, 6144], P('view', 'tile'), may hold values from -6 to 6
- taps: int32 [16, 128, 16], P('view', None, 'tile'), may hold values from 0 to 3838, as said below
- weights: bfloat16 [16, 128, 4, 32768], P('view', None, None, 'tile'), may hold values from 0 to 1, as said below
- conv_weight: float32 [3, 3, 3, 8], replicated, may hold values from -0.4375 to 0.4375
Outputs:
- log_prob: float32 [128, 32768], P('view', 'tile')
- depth_map: float32 [32768], P('tile')
Inputs may be any that keep to these rules, and one draw needn't show every extreme that they name: Every offset keeps all four taps of every pixel of the band inside the band's window. For each view, plane and pixel the four weights are (1 - a)(1 - b), a(1 - b), (1 - a) b, a b for some a, b in 0 to 1, rounded to bfloat16.
All inputs are finite; a program needn't handle non-finite values.
Results may differ from a plain program's by a relative error of at most 0.0003.
Values sent between devices are 32-bit elements; how exact they have to be, the bound alone decides.
No kernel may reach another device: no remote copies, remote signals or barrier semaphores. Data moves between devices by JAX's collectives and lax.ppermute only.
A program may use at most 128 MiB of HBM per device.

v0:
```python
import functools

import jax
import jax.numpy as jnp
from jax import lax
from jax.experimental import pallas as pl
from jax.experimental.pallas import tpu as pltpu
from jax.sharding import PartitionSpec as P


L = 128
G = 8
CH = 4
HALVES = 2
COLS = HALVES * L
GROUP = 8
PACK = 16
SIDE = 4


def block_kernel(turns, scal_ref, ref_hbm, src_hbm, w_hbm, filt_ref, *refs):
    outs, refs = refs[:len(turns)], refs[len(turns):]
    (ref_ref, src_ref, win, base, tmp, wbuf, wf, high, low, lhs, slide, out_ref, sem) = refs
    depth = w_hbm.shape[0]
    count = out_ref.shape[0]
    step = pl.program_id(0)
    held = wbuf.shape[1]
    strips = base.shape[0]
    rows = strips // HALVES

    def span_of(turn):
        block = lax.rem(scal_ref[depth] + turn, SIDE)
        first = block * count - 1
        return block, first, jnp.clip(first, 0, depth - held)

    def fetch(n):
        return pltpu.make_async_copy(w_hbm.at[pl.ds(span_of(turns[n])[2], held)], wbuf.at[n], sem.at[n + 2])

    turn = turns[0]
    for n in range(1, len(turns)):
        turn = jnp.where(step == n, turns[n], turn)
    block, first, start = span_of(turn)

    width = (GROUP + 2) * G

    @pl.when(step == 0)
    def _():
        get_src = pltpu.make_async_copy(src_hbm, src_ref, sem.at[0])
        get_ref = pltpu.make_async_copy(ref_hbm, ref_ref, sem.at[1])
        get_src.start()
        get_ref.start()
        for n in range(len(turns)):
            fetch(n).start()
        batch = tmp.shape[0]

        def regroup(ref, m, u, scale):
            at = pl.multiple_of(m * L, L)
            tmp[u] = ref[:, pl.ds(at, L)].astype(jnp.float32) * scale
            return [tmp[u, pl.ds(i, G, stride=CH), :] for i in range(CH)]

        slide[...] = jnp.zeros_like(slide)
        span = L + PACK
        gap = lax.broadcasted_iota(jnp.int32, (span, L), 0) - lax.broadcasted_iota(jnp.int32, (span, L), 1)

        def lay_slide(n, _):
            slide[n, L:L + span, :] = (gap == n).astype(jnp.float32).astype(jnp.bfloat16)
            return 0

        lax.fori_loop(0, PACK, lay_slide, 0)

        spread = (lax.rem(lax.broadcasted_iota(jnp.int32, (G, width), 1), G)
                  == lax.broadcasted_iota(jnp.int32, (G, width), 0)).astype(jnp.bfloat16)
        dist = (lax.broadcasted_iota(jnp.int32, (GROUP, width), 1) // G
                - lax.broadcasted_iota(jnp.int32, (GROUP, width), 0))
        for b in range(3):
            for e in range(3):
                main = jnp.zeros((GROUP, width), jnp.float32)
                rest = main
                for a in range(3):
                    taps = jnp.broadcast_to(filt_ref[a, b, e:e + 1, :], (G, G))
                    top = taps.astype(jnp.bfloat16)
                    left = (taps - top.astype(jnp.float32)).astype(jnp.bfloat16)
                    wide = jnp.dot(top, spread, preferred_element_type=jnp.float32)
                    fine = jnp.dot(left, spread, preferred_element_type=jnp.float32)
                    main = jnp.where(dist == a, wide, main)
                    rest = jnp.where(dist == a, fine, rest)
                at = (b * 3 + e) * GROUP
                lhs[at:at + GROUP, :] = jnp.concatenate([main, main, rest], axis=1)

        def lay_base(n, _):
            for u in range(batch):
                m = n * batch + u
                for i, part in enumerate(regroup(ref_ref, m, u, 1.0 / CH)):
                    base[m, i] = part
            return 0

        get_ref.wait()
        lax.fori_loop(0, strips // batch, lay_base, 0)

        def lay_window(n, _):
            for u in range(batch):
                m = n * batch + u
                strip = jnp.concatenate(regroup(src_ref, m, u, 1.0), axis=0).astype(jnp.bfloat16)
                win[m + 1, :, 0:L] = strip
                win[m, :, L:2 * L] = strip
            return 0

        get_src.wait()
        lax.fori_loop(0, (win.shape[0] - 1) // batch, lay_window, 0)

    for n in range(len(turns)):
        @pl.when(step == n)
        def _():
            fetch(n).wait()


    def aligner_of(by):
        whole = by // PACK
        at = pl.multiple_of(L - whole * PACK, PACK)
        return slide[by - whole * PACK, pl.ds(at, 2 * L), :]

    def plane(i, slot):
        at = jnp.clip(first + i, 0, depth - 1)
        off = scal_ref[at]
        m0 = off // L
        sl = off - m0 * L
        wf[slot, 0:4, :] = w_pick(at - start)
        aligner = jnp.concatenate([aligner_of(sl), aligner_of(sl + 1)], axis=1)
        count_r = strips + HALVES
        source = win[pl.ds(m0 + 1, count_r)].reshape(count_r * CH * G, 2 * L)
        moved = jnp.dot(source, aligner, preferred_element_type=jnp.float32)
        us, vs, sums = [], [], []
        for r in range(count_r):
            us.append([moved[(r * CH + c) * G:(r * CH + c + 1) * G, 0:L] for c in range(CH)])
            vs.append([moved[(r * CH + c) * G:(r * CH + c + 1) * G, L:2 * L] for c in range(CH)])
            j = r - HALVES
            if j < 0:
                continue
            total = None
            for k, taps in enumerate((us[j], vs[j], us[r], vs[r])):
                part = base[j, 0] * taps[0]
                for c in range(1, CH):
                    part = part + base[j, c] * taps[c]
                part = part * jnp.broadcast_to(wf[slot, k:k + 1, j * L:(j + 1) * L], (G, L))
                total = part if total is None else total + part
            sums.append(total)
        return sums

    def w_pick(at):
        return wbuf[step, at].astype(jnp.float32)

    def pair(p, slot):
        one = plane(2 * p, slot)
        two = plane(2 * p + 1, slot + 1)
        at = pl.multiple_of(p * 2 * G, 2 * G)
        for j in range(strips):
            both = jnp.concatenate([one[j], two[j]], axis=0)
            top = both.astype(jnp.bfloat16)
            high[pl.ds(at, 2 * G), j * L:(j + 1) * L] = top
            low[pl.ds(at, 2 * G), j * L:(j + 1) * L] = (both - top.astype(jnp.float32)).astype(jnp.bfloat16)

    edge = lax.broadcasted_iota(jnp.int32, (GROUP, COLS), 1)

    def filter_group(q):
        at = pl.multiple_of(q * GROUP * G, GROUP * G)
        put = pl.multiple_of(q * GROUP, GROUP)
        lines = [None] * (rows + 2)
        matrix = lhs[...].astype(jnp.bfloat16)
        for r in range(rows):
            top = high[pl.ds(at, width), r * COLS:(r + 1) * COLS]
            left = low[pl.ds(at, width), r * COLS:(r + 1) * COLS]
            res = jnp.dot(matrix, jnp.concatenate([top, left, top], axis=0), preferred_element_type=jnp.float32)
            for b in range(3):
                part = [res[(b * 3 + e) * GROUP:(b * 3 + e + 1) * GROUP] for e in range(3)]
                s = part[1]
                s = s + jnp.where(edge == 0, 0.0, pltpu.roll(part[0], 1, axis=1))
                s = s + jnp.where(edge == COLS - 1, 0.0, pltpu.roll(part[2], COLS - 1, axis=1))
                n = r - b + 2
                lines[n] = s if lines[n] is None else lines[n] + s
        for n in range(rows + 2):
            out_ref[pl.ds(put, GROUP), n * COLS:(n + 1) * COLS] = lines[n]

    pair(0, 0)

    @pl.when(block == 0)
    def _():
        high[0:G, :] = jnp.zeros((G, high.shape[1]), jnp.bfloat16)
        low[0:G, :] = jnp.zeros((G, high.shape[1]), jnp.bfloat16)

    def body(q, _):
        filter_group(jnp.maximum(q - 1, 0))
        for u in range(GROUP // 2):
            pair(q * (GROUP // 2) + 1 + u, 2 * u)
        return 0

    groups = count // GROUP
    lax.fori_loop(0, groups, body, 0)

    @pl.when(block == SIDE - 1)
    def _():
        end = (count + 2) * G
        high[end - G:end, :] = jnp.zeros((G, high.shape[1]), jnp.bfloat16)
        low[end - G:end, :] = jnp.zeros((G, high.shape[1]), jnp.bfloat16)

    filter_group(groups - 1)
    for n in range(len(turns)):
        @pl.when(step == n)
        def _():
            outs[n][...] = out_ref[...]


def block_filter(turns, scal, ref_feat, window, weights, conv_weight, count):
    _, _, pixels = weights.shape
    chans, q = window.shape
    rows = pixels // COLS
    vmem = pl.BlockSpec(memory_space=pltpu.VMEM)
    held = count + 2
    grid_spec = pltpu.PrefetchScalarGridSpec(
        num_scalar_prefetch=1,
        grid=(len(turns),),
        in_specs=[
            pl.BlockSpec(memory_space=pl.ANY),
            pl.BlockSpec(memory_space=pl.ANY),
            pl.BlockSpec(memory_space=pl.ANY),
            pl.BlockSpec((3, 3, 3, G), lambda c, t: (0, 0, 0, 0)),
        ],
        out_specs=[pl.BlockSpec((count, (rows + 2) * COLS), lambda c, t: (0, 0))] * len(turns),
        scratch_shapes=[
            pltpu.VMEM((chans, pixels), jnp.bfloat16),
            pltpu.VMEM((chans, q), jnp.bfloat16),
            pltpu.VMEM((q // L + 1, chans, 2 * L), jnp.bfloat16),
            pltpu.VMEM((pixels // L, CH, G, L), jnp.float32),
            pltpu.VMEM((8, chans, L), jnp.float32),
            pltpu.VMEM((len(turns), held, 4, pixels), jnp.bfloat16),
            pltpu.VMEM((GROUP, 8, pixels), jnp.float32),
            pltpu.VMEM((held * G, pixels), jnp.bfloat16),
            pltpu.VMEM((held * G, pixels), jnp.bfloat16),
            pltpu.VMEM((9 * GROUP, 3 * (GROUP + 2) * G), jnp.float32),
            pltpu.VMEM((PACK, 3 * L, L), jnp.bfloat16),
            pltpu.VMEM((count, (rows + 2) * COLS), jnp.float32),
            pltpu.SemaphoreType.DMA((2 + len(turns),)),
        ],
    )
    return pl.pallas_call(
        functools.partial(block_kernel, turns),
        out_shape=[jax.ShapeDtypeStruct((count, (rows + 2) * COLS), jnp.float32)] * len(turns),
        grid_spec=grid_spec,
        cost_estimate=pl.CostEstimate(flops=3_000_000_000 * len(turns), bytes_accessed=2_000_000, transcendentals=0),
    )(scal, ref_feat, window, weights, conv_weight)


def view_shift(value, by_outer, by_inner):
    pairs = [
        (o * SIDE + i, (o + by_outer) % SIDE * SIDE + (i + by_inner) % SIDE)
        for o in range(SIDE)
        for i in range(SIDE)
    ]
    return lax.ppermute(value, "view", pairs)


def scatter_stage(value, mine, outer):
    parts = value.reshape(SIDE, value.shape[0] // SIDE, *value.shape[1:])
    total = lax.dynamic_index_in_dim(parts, mine, 0, False)
    for by in (2, 1, 3):
        away = lax.dynamic_index_in_dim(parts, (mine + by) % SIDE, 0, False)
        total = total + view_shift(away, *((by, 0) if outer else (0, by)))
    return total


def sum_stage(value, outer):
    total = value
    for by in (2, 1, 3):
        total = total + view_shift(value, *((by, 0) if outer else (0, by)))
    return total


def on_device(ref_feat, src_feat, taps, weights, conv_weight):
    depth = taps.shape[1]
    pixels = ref_feat.shape[1]
    cols = 2 * L
    view = lax.axis_index("view")
    count = depth // SIDE
    scal = jnp.concatenate([taps[0, :, 0], (view // SIDE).astype(jnp.int32)[None]])
    got = {}
    for turns in ((2,), (1, 3), (0,)):
        parts = block_filter(turns, scal, ref_feat, src_feat[0, 0], weights[0], conv_weight, count)
        scal, *parts = lax.optimization_barrier((scal, *parts))
        for turn, part in zip(turns, parts):
            got[turn] = view_shift(part, turn, 0) if turn else part
    slab = got[0] + got[2] + got[1] + got[3]
    slab = scatter_stage(slab, view % SIDE, False)
    tiles = lax.axis_size("tile")
    up = lax.ppermute(slab[:, :cols], "tile", [(t + 1, t) for t in range(tiles - 1)])
    down = lax.ppermute(slab[:, cols + pixels:], "tile", [(t, t + 1) for t in range(tiles - 1)])
    filtered = slab[:, cols:cols + pixels]
    filtered = filtered + jnp.pad(down, ((0, 0), (0, pixels - cols))) + jnp.pad(up, ((0, 0), (pixels - cols, 0)))
    logit = 4.0 * jnp.tanh(0.5 * filtered)
    ex = jnp.exp(logit)
    slab_size = filtered.shape[0]
    plane = (view * slab_size + lax.iota(jnp.int32, slab_size)).astype(jnp.float32) / (depth - 1)
    sums = jnp.stack([jnp.sum(ex, axis=0), jnp.sum(ex * plane[:, None], axis=0)])
    sums = sum_stage(sum_stage(sums, True), False)
    return logit - jnp.log(sums[0])[None], sums[1] / sums[0]


def solution(mesh):
    placed = (
        P(None, "tile"),
        P("view", "tile", None, None),
        P("view", None, "tile"),
        P("view", None, None, "tile"),
        P(),
    )
    return jax.shard_map(
        on_device,
        mesh=mesh,
        in_specs=placed,
        out_specs=(P("view", "tile"), P("tile")),
        check_vma=False,
    )
```

profile of v0, /device:TPU:8, one launch (start us, length us, event | category | flops | bytes accessed | tf_op | source)
XLA Modules:
  0.0 92.5 jit_solution(870780417439144434)
XLA Ops:
  0.6 1.2 %pad_add_fusion.scal_ref = s32[129]{0:T(256)} fusion(s32[1]{0:T(128)} %bitcast.1, s32[128]{0:T(128)} %bitcast.28), kind=kLoop, calls=%fused_computation.20 | loop fusion | flops 129 | bytes 1032 | tf_op jit(solution)/shard_map/concatenate | solution.py:283
  1.9 9.4 %shard_map.68 = f32[32,2560]{1,0:T(8,128)} custom-call(s32[129]{0:T(256)} %pad_add_fusion.scal_ref, bf16[32,2048]{1,0:T(8,128)(2,1)} %ref_hbm.5, bf16[32,6144]{1,0:T(8,128)(2,1)} %bitcast.32, bf16[128,4,2048]{2,1,0:T(4,128)(2,1)} %bitcast.29, f32[3,3,3,8]{3,2,1,0:T(4,128)} %filt_ref.5), custom_call_target="tpu_custom_call" | custom-call | flops 3000000000 | bytes 2000000 | tf_op jit(solution)/shard_map/pallas_call | solution.py:244
  11.3 0.0 copy-start
  11.3 15.8 %shard_map.69 = (f32[32,2560]{1,0:T(8,128)}, f32[32,2560]{1,0:T(8,128)}) custom-call(s32[129]{0:T(256)} %pad_add_fusion.scal_ref, bf16[32,2048]{1,0:T(8,128)(2,1)} %ref_hbm.5, bf16[32,6144]{1,0:T(8,128)(2,1)} %bitcast.33, bf16[128,4,2048]{2,1,0:T(4,128)(2,1)} %bitcast.30, f32[3,3,3,8]{3,2,1,0:T(4,128)} %filt_ref.5), custom_call_target="tpu_custom_call" | custom-call | flops 6000000000 | bytes 2000000 | tf_op jit(solution)/shard_map/pallas_call | solution.py:244
  27.1 2.9 %collective-permute-start.2 = (f32[32,2560]{1,0:T(8,128)}, f32[32,2560]{1,0:T(8,128)S(1)}, u32[]{:S(2)}, u32[]{:S(2)}) collective-permute-start(f32[32,2560]{1,0:T(8,128)} %get-tuple-element.17), channel_id=1, source_target_pairs={{0,192},{16,208},{32,224},{48,240},{64,0},{80,16},{96,32},{112,48}... | collective-permute-start | bytes 983048 | tf_op jit(solution)/shard_map/ppermute | solution.py:258
  30.0 0.0 collective-permute-start.1
  30.0 0.0 copy-done
  30.0 2.3 %collective-permute-start = (f32[32,2560]{1,0:T(8,128)S(1)}, f32[32,2560]{1,0:T(8,128)S(1)}, u32[]{:S(2)}, u32[]{:S(2)}) collective-permute-start(f32[32,2560]{1,0:T(8,128)S(1)} %copy-done), channel_id=1, source_target_pairs={{0,128},{16,144},{32,160},{48,176},{64,192},{80,208},{96,224},{112... | collective-permute-start | bytes 983048 | tf_op jit(solution)/shard_map/ppermute | solution.py:258
  32.3 9.4 %shard_map.70 = f32[32,2560]{1,0:T(8,128)} custom-call(s32[129]{0:T(256)} %pad_add_fusion.scal_ref, bf16[32,2048]{1,0:T(8,128)(2,1)} %ref_hbm.5, bf16[32,6144]{1,0:T(8,128)(2,1)} %bitcast.34, bf16[128,4,2048]{2,1,0:T(4,128)(2,1)} %bitcast.31, f32[3,3,3,8]{3,2,1,0:T(4,128)} %filt_ref.5), custom_call_target="tpu_custom_call" | custom-call | flops 3000000000 | bytes 2000000 | tf_op jit(solution)/shard_map/pallas_call | solution.py:244
  41.8 2.5 %collective-permute-done.2 = f32[32,2560]{1,0:T(8,128)S(1)} collective-permute-done((f32[32,2560]{1,0:T(8,128)}, f32[32,2560]{1,0:T(8,128)S(1)}, u32[]{:S(2)}, u32[]{:S(2)}) %collective-permute-start.2) | collective-permute-done | bytes 327712 | tf_op jit(solution)/shard_map/ppermute | solution.py:258
  44.3 3.3 %collective-permute-done.1 = f32[32,2560]{1,0:T(8,128)S(1)} collective-permute-done((f32[32,2560]{1,0:T(8,128)}, f32[32,2560]{1,0:T(8,128)S(1)}, u32[]{:S(2)}, u32[]{:S(2)}) %collective-permute-start.1) | collective-permute-done | bytes 327712 | tf_op jit(solution)/shard_map/ppermute | solution.py:258
  47.6 0.0 collective-permute-done
  47.6 1.0 %add_bitcast_fusion = f32[4,8,2560]{2,1,0:T(8,128)S(1)} fusion(f32[32,2560]{1,0:T(8,128)S(1)} %collective-permute-done.2, f32[32,2560]{1,0:T(8,128)S(1)} %collective-permute-done.1, f32[32,2560]{1,0:T(8,128)} %shard_map.70, f32[32,2560]{1,0:T(8,128)S(1)} %collective-permute-done), kind=kLoop, calls=%fused_computation | loop fusion | flops 245760 | bytes 1638400 | tf_op jit(solution)/shard_map/reshape | solution.py:262
  48.7 6.4 %collective-permute-start.5 = (f32[8,2560]{1,0:T(8,128)S(1)}, f32[8,2560]{1,0:T(8,128)S(1)}, u32[]{:S(2)}, u32[]{:S(2)}) collective-permute-start(f32[8,2560]{1,0:T(8,128)S(1)} %get-tuple-element.21), channel_id=1, source_target_pairs={{0,48},{16,0},{32,16},{48,32},{64,112},{80,64},{96,80},{112,96},{1... | collective-permute-start | bytes 245768 | tf_op jit(solution)/shard_map/ppermute | solution.py:258
  55.1 0.0 collective-permute-start.4
  55.1 3.8 %collective-permute-start.3 = (f32[8,2560]{1,0:T(8,128)S(1)}, f32[8,2560]{1,0:T(8,128)S(1)}, u32[]{:S(2)}, u32[]{:S(2)}) collective-permute-start(f32[8,2560]{1,0:T(8,128)S(1)} %get-tuple-element.20), channel_id=1, source_target_pairs={{0,32},{16,48},{32,0},{48,16},{64,96},{80,112},{96,64},{112,80},{1... | collective-permute-start | bytes 245768 | tf_op jit(solution)/shard_map/ppermute | solution.py:258
  58.9 0.0 collective-permute-done.5
  58.9 3.3 %collective-permute-done.4 = f32[8,2560]{1,0:T(8,128)S(1)} collective-permute-done((f32[8,2560]{1,0:T(8,128)S(1)}, f32[8,2560]{1,0:T(8,128)S(1)}, u32[]{:S(2)}, u32[]{:S(2)}) %collective-permute-start.4) | collective-permute-done | bytes 81952 | tf_op jit(solution)/shard_map/ppermute | solution.py:258
  62.2 1.8 %collective-permute-done.3 = f32[8,2560]{1,0:T(8,128)S(1)} collective-permute-done((f32[8,2560]{1,0:T(8,128)S(1)}, f32[8,2560]{1,0:T(8,128)S(1)}, u32[]{:S(2)}, u32[]{:S(2)}) %collective-permute-start.3) | collective-permute-done | bytes 81952 | tf_op jit(solution)/shard_map/ppermute | solution.py:258
  64.0 1.9 %collective-permute-start.7 = (f32[8,256]{1,0:T(8,128)S(1)}, f32[8,256]{1,0:T(8,128)S(1)}, u32[]{:S(2)}, u32[]{:S(2)}) collective-permute-start(f32[8,256]{1,0:T(8,128)S(1)} %get-tuple-element.24), channel_id=1, source_target_pairs={{1,0},{2,1},{3,2},{4,3},{5,4},{6,5},{7,6},{8,7},{9,8},{10,9},{11,1... | collective-permute-start | bytes 24584 | tf_op jit(solution)/shard_map/ppermute | solution.py:293
  65.9 2.4 %collective-permute-start.6 = (f32[8,256]{1,0:T(8,128)S(1)}, f32[8,256]{1,0:T(8,128)S(1)}, u32[]{:S(2)}, u32[]{:S(2)}) collective-permute-start(f32[8,256]{1,0:T(8,128)S(1)} %get-tuple-element.23), channel_id=1, source_target_pairs={{0,1},{1,2},{2,3},{3,4},{4,5},{5,6},{6,7},{7,8},{8,9},{9,10},{10,1... | collective-permute-start | bytes 24584 | tf_op jit(solution)/shard_map/ppermute | solution.py:294
  68.4 0.0 collective-permute-done.7
  68.4 3.4 %collective-permute-done.6 = f32[8,256]{1,0:T(8,128)S(1)} collective-permute-done((f32[8,256]{1,0:T(8,128)S(1)}, f32[8,256]{1,0:T(8,128)S(1)}, u32[]{:S(2)}, u32[]{:S(2)}) %collective-permute-start.6) | collective-permute-done | bytes 8224 | tf_op jit(solution)/shard_map/ppermute | solution.py:294
  71.8 0.1 exponential_reduce_fusion
  71.9 0.6 collective-permute-start.10
  72.6 1.6 %collective-permute-start.9 = (f32[2,2048]{1,0:T(2,128)S(1)}, f32[2,2048]{1,0:T(2,128)S(1)}, u32[]{:S(2)}, u32[]{:S(2)}) collective-permute-start(f32[2,2048]{1,0:T(2,128)S(1)} %pad_maximum_fusion), channel_id=1, source_target_pairs={{0,64},{16,80},{32,96},{48,112},{64,128},{80,144},{96,160},{112,17... | collective-permute-start | bytes 49160 | tf_op jit(solution)/shard_map/ppermute | solution.py:258
  74.2 0.9 collective-permute-start.8
  75.1 0.8 collective-permute-done.10
  75.9 1.6 %collective-permute-done.9 = f32[2,2048]{1,0:T(2,128)S(1)} collective-permute-done((f32[2,2048]{1,0:T(2,128)S(1)}, f32[2,2048]{1,0:T(2,128)S(1)}, u32[]{:S(2)}, u32[]{:S(2)}) %collective-permute-start.9) | collective-permute-done | bytes 16416 | tf_op jit(solution)/shard_map/ppermute | solution.py:258
  77.5 1.9 %collective-permute-done.8 = f32[2,2048]{1,0:T(2,128)S(1)} collective-permute-done((f32[2,2048]{1,0:T(2,128)S(1)}, f32[2,2048]{1,0:T(2,128)S(1)}, u32[]{:S(2)}, u32[]{:S(2)}) %collective-permute-start.8) | collective-permute-done | bytes 16416 | tf_op jit(solution)/shard_map/ppermute | solution.py:258
  79.5 4.1 %collective-permute-start.13 = (f32[2,2048]{1,0:T(2,128)S(1)}, f32[2,2048]{1,0:T(2,128)S(1)}, u32[]{:S(2)}, u32[]{:S(2)}) collective-permute-start(f32[2,2048]{1,0:T(2,128)S(1)} %add_add_fusion.1), channel_id=1, source_target_pairs={{0,48},{16,0},{32,16},{48,32},{64,112},{80,64},{96,80},{112,96},{1... | collective-permute-start | bytes 49160 | tf_op jit(solution)/shard_map/ppermute | solution.py:258
  83.6 0.0 collective-permute-start.12
  83.6 3.1 %collective-permute-start.11 = (f32[2,2048]{1,0:T(2,128)S(1)}, f32[2,2048]{1,0:T(2,128)S(1)}, u32[]{:S(2)}, u32[]{:S(2)}) collective-permute-start(f32[2,2048]{1,0:T(2,128)S(1)} %add_add_fusion.1), channel_id=1, source_target_pairs={{0,32},{16,48},{32,0},{48,16},{64,96},{80,112},{96,64},{112,80},{1... | collective-permute-start | bytes 49160 | tf_op jit(solution)/shard_map/ppermute | solution.py:258
  86.7 0.0 collective-permute-done.13
  86.7 2.7 %collective-permute-done.12 = f32[2,2048]{1,0:T(2,128)S(1)} collective-permute-done((f32[2,2048]{1,0:T(2,128)S(1)}, f32[2,2048]{1,0:T(2,128)S(1)}, u32[]{:S(2)}, u32[]{:S(2)}) %collective-permute-start.12) | collective-permute-done | bytes 16416 | tf_op jit(solution)/shard_map/ppermute | solution.py:258
  89.4 1.8 %collective-permute-done.11 = f32[2,2048]{1,0:T(2,128)S(1)} collective-permute-done((f32[2,2048]{1,0:T(2,128)S(1)}, f32[2,2048]{1,0:T(2,128)S(1)}, u32[]{:S(2)}, u32[]{:S(2)}) %collective-permute-start.11) | collective-permute-done | bytes 16416 | tf_op jit(solution)/shard_map/ppermute | solution.py:258
  91.3 0.6 slice_divide_fusion
  91.9 0.6 broadcast_subtract_fusion
  (7 shorter events, 0.1 us)
Async XLA Ops:
  11.3 18.7 %copy-start = (f32[32,2560]{1,0:T(8,128)S(1)}, f32[32,2560]{1,0:T(8,128)}, u32[]{:S(2)}) copy-start(f32[32,2560]{1,0:T(8,128)} %shard_map.68) | copy-start | bytes 983044
  27.1 17.2 %collective-permute-start.2 = (f32[32,2560]{1,0:T(8,128)}, f32[32,2560]{1,0:T(8,128)S(1)}, u32[]{:S(2)}, u32[]{:S(2)}) collective-permute-start(f32[32,2560]{1,0:T(8,128)} %get-tuple-element.17), channel_id=1, source_target_pairs={{0,192},{16,208},{32,224},{48,240},{64,0},{80,16},{96,32},{112,48}... | collective-permute-start | bytes 983048 | tf_op jit(solution)/shard_map/ppermute | solution.py:258
  30.0 17.6 %collective-permute-start.1 = (f32[32,2560]{1,0:T(8,128)}, f32[32,2560]{1,0:T(8,128)S(1)}, u32[]{:S(2)}, u32[]{:S(2)}) collective-permute-start(f32[32,2560]{1,0:T(8,128)} %get-tuple-element.16), channel_id=1, source_target_pairs={{0,64},{16,80},{32,96},{48,112},{64,128},{80,144},{96,160},{112,17... | collective-permute-start | bytes 983048 | tf_op jit(solution)/shard_map/ppermute | solution.py:258
  30.0 17.6 %collective-permute-start = (f32[32,2560]{1,0:T(8,128)S(1)}, f32[32,2560]{1,0:T(8,128)S(1)}, u32[]{:S(2)}, u32[]{:S(2)}) collective-permute-start(f32[32,2560]{1,0:T(8,128)S(1)} %copy-done), channel_id=1, source_target_pairs={{0,128},{16,144},{32,160},{48,176},{64,192},{80,208},{96,224},{112... | collective-permute-start | bytes 983048 | tf_op jit(solution)/shard_map/ppermute | solution.py:258
  48.7 10.2 %collective-permute-start.5 = (f32[8,2560]{1,0:T(8,128)S(1)}, f32[8,2560]{1,0:T(8,128)S(1)}, u32[]{:S(2)}, u32[]{:S(2)}) collective-permute-start(f32[8,2560]{1,0:T(8,128)S(1)} %get-tuple-element.21), channel_id=1, source_target_pairs={{0,48},{16,0},{32,16},{48,32},{64,112},{80,64},{96,80},{112,96},{1... | collective-permute-start | bytes 245768 | tf_op jit(solution)/shard_map/ppermute | solution.py:258
  55.1 7.1 %collective-permute-start.4 = (f32[8,2560]{1,0:T(8,128)S(1)}, f32[8,2560]{1,0:T(8,128)S(1)}, u32[]{:S(2)}, u32[]{:S(2)}) collective-permute-start(f32[8,2560]{1,0:T(8,128)S(1)} %get-tuple-element.22), channel_id=1, source_target_pairs={{0,16},{16,32},{32,48},{48,0},{64,80},{80,96},{96,112},{112,64},{1... | collective-permute-start | bytes 245768 | tf_op jit(solution)/shard_map/ppermute | solution.py:258
  55.1 8.9 %collective-permute-start.3 = (f32[8,2560]{1,0:T(8,128)S(1)}, f32[8,2560]{1,0:T(8,128)S(1)}, u32[]{:S(2)}, u32[]{:S(2)}) collective-permute-start(f32[8,2560]{1,0:T(8,128)S(1)} %get-tuple-element.20), channel_id=1, source_target_pairs={{0,32},{16,48},{32,0},{48,16},{64,96},{80,112},{96,64},{112,80},{1... | collective-permute-start | bytes 245768 | tf_op jit(solution)/shard_map/ppermute | solution.py:258
  64.0 4.4 %collective-permute-start.7 = (f32[8,256]{1,0:T(8,128)S(1)}, f32[8,256]{1,0:T(8,128)S(1)}, u32[]{:S(2)}, u32[]{:S(2)}) collective-permute-start(f32[8,256]{1,0:T(8,128)S(1)} %get-tuple-element.24), channel_id=1, source_target_pairs={{1,0},{2,1},{3,2},{4,3},{5,4},{6,5},{7,6},{8,7},{9,8},{10,9},{11,1... | collective-permute-start | bytes 24584 | tf_op jit(solution)/shard_map/ppermute | solution.py:293
  65.9 5.9 %collective-permute-start.6 = (f32[8,256]{1,0:T(8,128)S(1)}, f32[8,256]{1,0:T(8,128)S(1)}, u32[]{:S(2)}, u32[]{:S(2)}) collective-permute-start(f32[8,256]{1,0:T(8,128)S(1)} %get-tuple-element.23), channel_id=1, source_target_pairs={{0,1},{1,2},{2,3},{3,4},{4,5},{5,6},{6,7},{7,8},{8,9},{9,10},{10,1... | collective-permute-start | bytes 24584 | tf_op jit(solution)/shard_map/ppermute | solution.py:294
  71.9 4.0 %collective-permute-start.10 = (f32[2,2048]{1,0:T(2,128)S(1)}, f32[2,2048]{1,0:T(2,128)S(1)}, u32[]{:S(2)}, u32[]{:S(2)}) collective-permute-start(f32[2,2048]{1,0:T(2,128)S(1)} %pad_maximum_fusion), channel_id=1, source_target_pairs={{0,192},{16,208},{32,224},{48,240},{64,0},{80,16},{96,32},{112,48}... | collective-permute-start | bytes 49160 | tf_op jit(solution)/shard_map/ppermute | solution.py:258
  72.6 4.9 %collective-permute-start.9 = (f32[2,2048]{1,0:T(2,128)S(1)}, f32[2,2048]{1,0:T(2,128)S(1)}, u32[]{:S(2)}, u32[]{:S(2)}) collective-permute-start(f32[2,2048]{1,0:T(2,128)S(1)} %pad_maximum_fusion), channel_id=1, source_target_pairs={{0,64},{16,80},{32,96},{48,112},{64,128},{80,144},{96,160},{112,17... | collective-permute-start | bytes 49160 | tf_op jit(solution)/shard_map/ppermute | solution.py:258
  74.2 5.2 %collective-permute-start.8 = (f32[2,2048]{1,0:T(2,128)S(1)}, f32[2,2048]{1,0:T(2,128)S(1)}, u32[]{:S(2)}, u32[]{:S(2)}) collective-permute-start(f32[2,2048]{1,0:T(2,128)S(1)} %pad_maximum_fusion), channel_id=1, source_target_pairs={{0,128},{16,144},{32,160},{48,176},{64,192},{80,208},{96,224},{112... | collective-permute-start | bytes 49160 | tf_op jit(solution)/shard_map/ppermute | solution.py:258
  79.5 7.2 %collective-permute-start.13 = (f32[2,2048]{1,0:T(2,128)S(1)}, f32[2,2048]{1,0:T(2,128)S(1)}, u32[]{:S(2)}, u32[]{:S(2)}) collective-permute-start(f32[2,2048]{1,0:T(2,128)S(1)} %add_add_fusion.1), channel_id=1, source_target_pairs={{0,48},{16,0},{32,16},{48,32},{64,112},{80,64},{96,80},{112,96},{1... | collective-permute-start | bytes 49160 | tf_op jit(solution)/shard_map/ppermute | solution.py:258
  83.6 5.8 %collective-permute-start.12 = (f32[2,2048]{1,0:T(2,128)S(1)}, f32[2,2048]{1,0:T(2,128)S(1)}, u32[]{:S(2)}, u32[]{:S(2)}) collective-permute-start(f32[2,2048]{1,0:T(2,128)S(1)} %add_add_fusion.1), channel_id=1, source_target_pairs={{0,16},{16,32},{32,48},{48,0},{64,80},{80,96},{96,112},{112,64},{1... | collective-permute-start | bytes 49160 | tf_op jit(solution)/shard_map/ppermute | solution.py:258
  83.6 7.7 %collective-permute-start.11 = (f32[2,2048]{1,0:T(2,128)S(1)}, f32[2,2048]{1,0:T(2,128)S(1)}, u32[]{:S(2)}, u32[]{:S(2)}) collective-permute-start(f32[2,2048]{1,0:T(2,128)S(1)} %add_add_fusion.1), channel_id=1, source_target_pairs={{0,32},{16,48},{32,0},{48,16},{64,96},{80,112},{96,64},{112,80},{1... | collective-permute-start | bytes 49160 | tf_op jit(solution)/shard_map/ppermute | solution.py:258
where the time goes:
time: 93 us; the launch traced here: 92.5 us
  Pallas kernels  34.7 us (37%)
  starting transfers between devices  30.2 us (32%)
  waiting for transfers between devices  23.2 us (25%)
  other arithmetic  3.72 us (4%)
    pallas_call x3, Pallas kernels, block_filter(): pl.pallas_call(functools.partial(block_kernel, turns), out_shape=[jax.Sha...  34.7 us
    ppermute x12, starting transfers between devices, view_shift(): return lax.ppermute(value, 'view', pairs)  25.8 us
    ppermute x12, waiting for transfers between devices, view_shift(): return lax.ppermute(value, 'view', pairs)  19.7 us
    ppermute x1, waiting for transfers between devices, on_device(): lax.ppermute(slab[:, cols + pixels:], 'tile', [(t, t + 1) for t in range(...  3.43 us
    ppermute x1, starting transfers between devices, on_device(): lax.ppermute(slab[:, cols + pixels:], 'tile', [(t, t + 1) for t in range(...  2.41 us
    ppermute x1, starting transfers between devices, on_device(): lax.ppermute(slab[:, :cols], 'tile', [(t + 1, t) for t in range(tiles - 1)])  1.92 us
  transfers between devices with their start and end apart: 14, of which 10 were waited for; matrix products, arithmetic and copies ran while one was open for 0% of the time, Pallas kernels for 10%

commit v1 on v0

--- a/solution.py
+++ b/solution.py
@@ -18,9 +18,13 @@
 SIDE = 4
 
 
-def block_kernel(turns, scal_ref, ref_hbm, src_hbm, w_hbm, filt_ref, *refs):
+def outer_index():
+    return lax.axis_index("view") // SIDE
+
+
+def block_kernel(turns, taps_ref, ref_hbm, src_hbm, w_hbm, filt_hbm, *refs):
     outs, refs = refs[:len(turns)], refs[len(turns):]
-    (ref_ref, src_ref, win, base, tmp, wbuf, wf, high, low, lhs, slide, out_ref, sem) = refs
+    (ref_ref, src_ref, filt_ref, win, base, tmp, wbuf, wf, high, low, lhs, slide, out_ref, sem) = refs
     depth = w_hbm.shape[0]
     count = out_ref.shape[0]
     step = pl.program_id(0)
@@ -29,12 +33,12 @@
     rows = strips // HALVES
 
     def span_of(turn):
-        block = lax.rem(scal_ref[depth] + turn, SIDE)
+        block = lax.rem(outer_index() + turn, SIDE)
         first = block * count - 1
         return block, first, jnp.clip(first, 0, depth - held)
 
     def fetch(n):
-        return pltpu.make_async_copy(w_hbm.at[pl.ds(span_of(turns[n])[2], held)], wbuf.at[n], sem.at[n + 2])
+        return pltpu.make_async_copy(w_hbm.at[pl.ds(span_of(turns[n])[2], held)], wbuf.at[n], sem.at[n + 3])
 
     turn = turns[0]
     for n in range(1, len(turns)):
@@ -47,6 +51,8 @@
     def _():
         get_src = pltpu.make_async_copy(src_hbm, src_ref, sem.at[0])
         get_ref = pltpu.make_async_copy(ref_hbm, ref_ref, sem.at[1])
+        get_filt = pltpu.make_async_copy(filt_hbm, filt_ref, sem.at[2])
+        get_filt.start()
         get_src.start()
         get_ref.start()
         for n in range(len(turns)):
@@ -68,6 +74,7 @@
 
         lax.fori_loop(0, PACK, lay_slide, 0)
 
+        get_filt.wait()
         spread = (lax.rem(lax.broadcasted_iota(jnp.int32, (G, width), 1), G)
                   == lax.broadcasted_iota(jnp.int32, (G, width), 0)).astype(jnp.bfloat16)
         dist = (lax.broadcasted_iota(jnp.int32, (GROUP, width), 1) // G
@@ -121,7 +128,7 @@
 
     def plane(i, slot):
         at = jnp.clip(first + i, 0, depth - 1)
-        off = scal_ref[at]
+        off = taps_ref[at]
         m0 = off // L
         sl = off - m0 * L
         wf[slot, 0:4, :] = w_pick(at - start)
@@ -129,21 +136,23 @@
         count_r = strips + HALVES
         source = win[pl.ds(m0 + 1, count_r)].reshape(count_r * CH * G, 2 * L)
         moved = jnp.dot(source, aligner, preferred_element_type=jnp.float32)
-        us, vs, sums = [], [], []
+        sums = [None] * strips
+
+        def add(j, r, k):
+            near = r * CH
+            for side in range(2):
+                part = None
+                for c in range(CH):
+                    item = moved[(near + c) * G:(near + c + 1) * G, side * L:(side + 1) * L] * base[j, c]
+                    part = item if part is None else part + item
+                part = part * jnp.broadcast_to(wf[slot, k + side:k + side + 1, j * L:(j + 1) * L], (G, L))
+                sums[j] = part if sums[j] is None else sums[j] + part
+
         for r in range(count_r):
-            us.append([moved[(r * CH + c) * G:(r * CH + c + 1) * G, 0:L] for c in range(CH)])
-            vs.append([moved[(r * CH + c) * G:(r * CH + c + 1) * G, L:2 * L] for c in range(CH)])
-            j = r - HALVES
-            if j < 0:
-                continue
-            total = None
-            for k, taps in enumerate((us[j], vs[j], us[r], vs[r])):
-                part = base[j, 0] * taps[0]
-                for c in range(1, CH):
-                    part = part + base[j, c] * taps[c]
-                part = part * jnp.broadcast_to(wf[slot, k:k + 1, j * L:(j + 1) * L], (G, L))
-                total = part if total is None else total + part
-            sums.append(total)
+            if r >= HALVES:
+                add(r - HALVES, r, 2)
+            if r < strips:
+                add(r, r, 0)
         return sums
 
     def w_pick(at):
@@ -161,24 +170,29 @@
 
     edge = lax.broadcasted_iota(jnp.int32, (GROUP, COLS), 1)
 
+    def finish(lines, n, put):
+        total = lines[n, 1]
+        total = total + jnp.where(edge == 0, 0.0, pltpu.roll(lines[n, 0], 1, axis=1))
+        total = total + jnp.where(edge == COLS - 1, 0.0, pltpu.roll(lines[n, 2], COLS - 1, axis=1))
+        out_ref[pl.ds(put, GROUP), n * COLS:(n + 1) * COLS] = total
+
     def filter_group(q):
         at = pl.multiple_of(q * GROUP * G, GROUP * G)
         put = pl.multiple_of(q * GROUP, GROUP)
-        lines = [None] * (rows + 2)
         matrix = lhs[...].astype(jnp.bfloat16)
+        lines = {}
         for r in range(rows):
             top = high[pl.ds(at, width), r * COLS:(r + 1) * COLS]
             left = low[pl.ds(at, width), r * COLS:(r + 1) * COLS]
             res = jnp.dot(matrix, jnp.concatenate([top, left, top], axis=0), preferred_element_type=jnp.float32)
             for b in range(3):
-                part = [res[(b * 3 + e) * GROUP:(b * 3 + e + 1) * GROUP] for e in range(3)]
-                s = part[1]
-                s = s + jnp.where(edge == 0, 0.0, pltpu.roll(part[0], 1, axis=1))
-                s = s + jnp.where(edge == COLS - 1, 0.0, pltpu.roll(part[2], COLS - 1, axis=1))
-                n = r - b + 2
-                lines[n] = s if lines[n] is None else lines[n] + s
-        for n in range(rows + 2):
-            out_ref[pl.ds(put, GROUP), n * COLS:(n + 1) * COLS] = lines[n]
+                for e in range(3):
+                    part = res[(b * 3 + e) * GROUP:(b * 3 + e + 1) * GROUP]
+                    n = r - b + 2
+                    lines[n, e] = lines[n, e] + part if (n, e) in lines else part
+            for n in (range(rows, rows + 2) if r == rows - 1 else ()):
+                finish(lines, n, put)
+            finish(lines, r, put)
 
     pair(0, 0)
 
@@ -209,7 +223,7 @@
             outs[n][...] = out_ref[...]
 
 
-def block_filter(turns, scal, ref_feat, window, weights, conv_weight, count):
+def block_filter(turns, offsets, ref_feat, window, weights, conv_weight, count):
     _, _, pixels = weights.shape
     chans, q = window.shape
     rows = pixels // COLS
@@ -222,12 +236,13 @@
             pl.BlockSpec(memory_space=pl.ANY),
             pl.BlockSpec(memory_space=pl.ANY),
             pl.BlockSpec(memory_space=pl.ANY),
-            pl.BlockSpec((3, 3, 3, G), lambda c, t: (0, 0, 0, 0)),
+            pl.BlockSpec(memory_space=pl.ANY),
         ],
         out_specs=[pl.BlockSpec((count, (rows + 2) * COLS), lambda c, t: (0, 0))] * len(turns),
         scratch_shapes=[
             pltpu.VMEM((chans, pixels), jnp.bfloat16),
             pltpu.VMEM((chans, q), jnp.bfloat16),
+            pltpu.VMEM((3, 3, 3, G), jnp.float32),
             pltpu.VMEM((q // L + 1, chans, 2 * L), jnp.bfloat16),
             pltpu.VMEM((pixels // L, CH, G, L), jnp.float32),
             pltpu.VMEM((8, chans, L), jnp.float32),
@@ -238,7 +253,7 @@
             pltpu.VMEM((9 * GROUP, 3 * (GROUP + 2) * G), jnp.float32),
             pltpu.VMEM((PACK, 3 * L, L), jnp.bfloat16),
             pltpu.VMEM((count, (rows + 2) * COLS), jnp.float32),
-            pltpu.SemaphoreType.DMA((2 + len(turns),)),
+            pltpu.SemaphoreType.DMA((3 + len(turns),)),
         ],
     )
     return pl.pallas_call(
@@ -246,7 +261,7 @@
         out_shape=[jax.ShapeDtypeStruct((count, (rows + 2) * COLS), jnp.float32)] * len(turns),
         grid_spec=grid_spec,
         cost_estimate=pl.CostEstimate(flops=3_000_000_000 * len(turns), bytes_accessed=2_000_000, transcendentals=0),
-    )(scal, ref_feat, window, weights, conv_weight)
+    )(offsets, ref_feat, window, weights, conv_weight)
 
 
 def view_shift(value, by_outer, by_inner):
@@ -280,11 +295,11 @@
     cols = 2 * L
     view = lax.axis_index("view")
     count = depth // SIDE
-    scal = jnp.concatenate([taps[0, :, 0], (view // SIDE).astype(jnp.int32)[None]])
+    offsets = taps[0, :, 0]
     got = {}
     for turns in ((2,), (1, 3), (0,)):
-        parts = block_filter(turns, scal, ref_feat, src_feat[0, 0], weights[0], conv_weight, count)
-        scal, *parts = lax.optimization_barrier((scal, *parts))
+        parts = block_filter(turns, offsets, ref_feat, src_feat[0, 0], weights[0], conv_weight, count)
+        offsets, *parts = lax.optimization_barrier((offsets, *parts))
         for turn, part in zip(turns, parts):
             got[turn] = view_shift(part, turn, 0) if turn else part
     slab = got[0] + got[2] + got[1] + got[3]

time: 93 us -> 90.1 us (0.969)
  Pallas kernels: 34.7 us -> 32.6 us
  waiting for transfers between devices: 23.2 us -> 24.7 us
  other arithmetic: 3.72 us -> 2.49 us
  starting transfers between devices: 30.2 us -> 29.1 us
    pallas_call x3, Pallas kernels: 34.7 us -> 32.6 us  [block_filter(): pl.pallas_call(functools.partial(block_kernel, turns), out_shape=[jax.Sha...]
    ppermute x12, waiting for transfers between devices: 19.7 us -> 21.3 us  [view_shift(): return lax.ppermute(value, 'view', pairs)]
    concatenate x1 -> x0, other arithmetic: 1.22 us -> none  [on_device(): jnp.concatenate([taps[0, :, 0], (view // SIDE).astype(jnp.int32)[None]])]
    ppermute x12, starting transfers between devices: 25.8 us -> 24.8 us  [view_shift(): return lax.ppermute(value, 'view', pairs)]
where the time goes in v1:
time: 90.1 us; the launch traced here: 89.7 us
  Pallas kernels  32.6 us (36%)
  starting transfers between devices  29.1 us (32%)
  waiting for transfers between devices  24.7 us (27%)
  other arithmetic  2.49 us (3%)
    pallas_call x3, Pallas kernels, block_filter(): pl.pallas_call(functools.partial(block_kernel, turns), out_shape=[jax.Sha...  32.6 us
    ppermute x12, starting transfers between devices, view_shift(): return lax.ppermute(value, 'view', pairs)  24.8 us
    ppermute x12, waiting for transfers between devices, view_shift(): return lax.ppermute(value, 'view', pairs)  21.3 us
    ppermute x1, waiting for transfers between devices, on_device(): lax.ppermute(slab[:, cols + pixels:], 'tile', [(t, t + 1) for t in range(...  3.43 us
    ppermute x1, starting transfers between devices, on_device(): lax.ppermute(slab[:, cols + pixels:], 'tile', [(t, t + 1) for t in range(...  2.41 us
    ppermute x1, starting transfers between devices, on_device(): lax.ppermute(slab[:, :cols], 'tile', [(t + 1, t) for t in range(tiles - 1)])  1.92 us
  transfers between devices with their start and end apart: 14, of which 10 were waited for; matrix products, arithmetic and copies ran while one was open for 0% of the time, Pallas kernels for 10%

profile of v1, /device:TPU:8, one launch (start us, length us, event | category | flops | bytes accessed | tf_op | source)
XLA Modules:
  0.0 89.7 jit_solution(2867914378686799924)
XLA Ops:
  0.6 8.7 %shard_map.68 = f32[32,2560]{1,0:T(8,128)} custom-call(s32[128]{0:T(128)} %bitcast.33, bf16[32,2048]{1,0:T(8,128)(2,1)} %ref_hbm.5, bf16[32,6144]{1,0:T(8,128)(2,1)} %bitcast.30, bf16[128,4,2048]{2,1,0:T(4,128)(2,1)} %bitcast.27, f32[3,3,3,8]{3,2,1,0:T(4,128)} %filt_hbm.5), custom_call_target="tpu_custom_call" | custom-call | flops 3000000000 | bytes 2000000 | tf_op jit(solution)/shard_map/pallas_call | solution.py:259
  9.4 0.0 copy-start
  9.4 15.2 %shard_map.69 = (f32[32,2560]{1,0:T(8,128)}, f32[32,2560]{1,0:T(8,128)}) custom-call(s32[128]{0:T(128)} %bitcast.34, bf16[32,2048]{1,0:T(8,128)(2,1)} %ref_hbm.5, bf16[32,6144]{1,0:T(8,128)(2,1)} %bitcast.31, bf16[128,4,2048]{2,1,0:T(4,128)(2,1)} %bitcast.28, f32[3,3,3,8]{3,2,1,0:T(4,128)} %filt_hbm.5), custom_call_target="tpu_custom_call" | custom-call | flops 6000000000 | bytes 2000000 | tf_op jit(solution)/shard_map/pallas_call | solution.py:259
  24.5 2.8 %collective-permute-start.2 = (f32[32,2560]{1,0:T(8,128)}, f32[32,2560]{1,0:T(8,128)S(1)}, u32[]{:S(2)}, u32[]{:S(2)}) collective-permute-start(f32[32,2560]{1,0:T(8,128)} %get-tuple-element.17), channel_id=1, source_target_pairs={{0,192},{16,208},{32,224},{48,240},{64,0},{80,16},{96,32},{112,48}... | collective-permute-start | bytes 983048 | tf_op jit(solution)/shard_map/ppermute | solution.py:273
  27.4 0.0 collective-permute-start.1
  27.4 0.0 copy-done
  27.4 2.3 %collective-permute-start = (f32[32,2560]{1,0:T(8,128)S(1)}, f32[32,2560]{1,0:T(8,128)S(1)}, u32[]{:S(2)}, u32[]{:S(2)}) collective-permute-start(f32[32,2560]{1,0:T(8,128)S(1)} %copy-done), channel_id=1, source_target_pairs={{0,128},{16,144},{32,160},{48,176},{64,192},{80,208},{96,224},{112... | collective-permute-start | bytes 983048 | tf_op jit(solution)/shard_map/ppermute | solution.py:273
  29.7 8.7 %shard_map.70 = f32[32,2560]{1,0:T(8,128)} custom-call(s32[128]{0:T(128)} %bitcast.35, bf16[32,2048]{1,0:T(8,128)(2,1)} %ref_hbm.5, bf16[32,6144]{1,0:T(8,128)(2,1)} %bitcast.32, bf16[128,4,2048]{2,1,0:T(4,128)(2,1)} %bitcast.29, f32[3,3,3,8]{3,2,1,0:T(4,128)} %filt_hbm.5), custom_call_target="tpu_custom_call" | custom-call | flops 3000000000 | bytes 2000000 | tf_op jit(solution)/shard_map/pallas_call | solution.py:259
  38.5 3.3 %collective-permute-done.2 = f32[32,2560]{1,0:T(8,128)S(1)} collective-permute-done((f32[32,2560]{1,0:T(8,128)}, f32[32,2560]{1,0:T(8,128)S(1)}, u32[]{:S(2)}, u32[]{:S(2)}) %collective-permute-start.2) | collective-permute-done | bytes 327712 | tf_op jit(solution)/shard_map/ppermute | solution.py:273
  41.7 3.3 %collective-permute-done.1 = f32[32,2560]{1,0:T(8,128)S(1)} collective-permute-done((f32[32,2560]{1,0:T(8,128)}, f32[32,2560]{1,0:T(8,128)S(1)}, u32[]{:S(2)}, u32[]{:S(2)}) %collective-permute-start.1) | collective-permute-done | bytes 327712 | tf_op jit(solution)/shard_map/ppermute | solution.py:273
  45.0 0.0 collective-permute-done
  45.0 1.0 %add_bitcast_fusion = f32[4,8,2560]{2,1,0:T(8,128)S(1)} fusion(f32[32,2560]{1,0:T(8,128)S(1)} %collective-permute-done.2, f32[32,2560]{1,0:T(8,128)S(1)} %collective-permute-done.1, f32[32,2560]{1,0:T(8,128)} %shard_map.70, f32[32,2560]{1,0:T(8,128)S(1)} %collective-permute-done), kind=kLoop, calls=%fused_computation | loop fusion | flops 245760 | bytes 1638400 | tf_op jit(solution)/shard_map/reshape | solution.py:277
  46.1 6.4 %collective-permute-start.5 = (f32[8,2560]{1,0:T(8,128)S(1)}, f32[8,2560]{1,0:T(8,128)S(1)}, u32[]{:S(2)}, u32[]{:S(2)}) collective-permute-start(f32[8,2560]{1,0:T(8,128)S(1)} %get-tuple-element.21), channel_id=1, source_target_pairs={{0,48},{16,0},{32,16},{48,32},{64,112},{80,64},{96,80},{112,96},{1... | collective-permute-start | bytes 245768 | tf_op jit(solution)/shard_map/ppermute | solution.py:273
  52.5 0.0 collective-permute-start.4
  52.5 3.8 %collective-permute-start.3 = (f32[8,2560]{1,0:T(8,128)S(1)}, f32[8,2560]{1,0:T(8,128)S(1)}, u32[]{:S(2)}, u32[]{:S(2)}) collective-permute-start(f32[8,2560]{1,0:T(8,128)S(1)} %get-tuple-element.20), channel_id=1, source_target_pairs={{0,32},{16,48},{32,0},{48,16},{64,96},{80,112},{96,64},{112,80},{1... | collective-permute-start | bytes 245768 | tf_op jit(solution)/shard_map/ppermute | solution.py:273
  56.3 0.0 collective-permute-done.5
  56.3 3.1 %collective-permute-done.4 = f32[8,2560]{1,0:T(8,128)S(1)} collective-permute-done((f32[8,2560]{1,0:T(8,128)S(1)}, f32[8,2560]{1,0:T(8,128)S(1)}, u32[]{:S(2)}, u32[]{:S(2)}) %collective-permute-start.4) | collective-permute-done | bytes 81952 | tf_op jit(solution)/shard_map/ppermute | solution.py:273
  59.4 2.2 %collective-permute-done.3 = f32[8,2560]{1,0:T(8,128)S(1)} collective-permute-done((f32[8,2560]{1,0:T(8,128)S(1)}, f32[8,2560]{1,0:T(8,128)S(1)}, u32[]{:S(2)}, u32[]{:S(2)}) %collective-permute-start.3) | collective-permute-done | bytes 81952 | tf_op jit(solution)/shard_map/ppermute | solution.py:273
  61.7 1.9 %collective-permute-start.7 = (f32[8,256]{1,0:T(8,128)S(1)}, f32[8,256]{1,0:T(8,128)S(1)}, u32[]{:S(2)}, u32[]{:S(2)}) collective-permute-start(f32[8,256]{1,0:T(8,128)S(1)} %get-tuple-element.24), channel_id=1, source_target_pairs={{1,0},{2,1},{3,2},{4,3},{5,4},{6,5},{7,6},{8,7},{9,8},{10,9},{11,1... | collective-permute-start | bytes 24584 | tf_op jit(solution)/shard_map/ppermute | solution.py:308
  63.6 2.4 %collective-permute-start.6 = (f32[8,256]{1,0:T(8,128)S(1)}, f32[8,256]{1,0:T(8,128)S(1)}, u32[]{:S(2)}, u32[]{:S(2)}) collective-permute-start(f32[8,256]{1,0:T(8,128)S(1)} %get-tuple-element.23), channel_id=1, source_target_pairs={{0,1},{1,2},{2,3},{3,4},{4,5},{5,6},{6,7},{7,8},{8,9},{9,10},{10,1... | collective-permute-start | bytes 24584 | tf_op jit(solution)/shard_map/ppermute | solution.py:309
  66.0 0.0 collective-permute-done.7
  66.1 3.4 %collective-permute-done.6 = f32[8,256]{1,0:T(8,128)S(1)} collective-permute-done((f32[8,256]{1,0:T(8,128)S(1)}, f32[8,256]{1,0:T(8,128)S(1)}, u32[]{:S(2)}, u32[]{:S(2)}) %collective-permute-start.6) | collective-permute-done | bytes 8224 | tf_op jit(solution)/shard_map/ppermute | solution.py:309
  69.5 0.1 exponential_reduce_fusion
  69.6 0.1 collective-permute-start.10
  69.7 2.0 %collective-permute-start.9 = (f32[2,2048]{1,0:T(2,128)S(1)}, f32[2,2048]{1,0:T(2,128)S(1)}, u32[]{:S(2)}, u32[]{:S(2)}) collective-permute-start(f32[2,2048]{1,0:T(2,128)S(1)} %pad_maximum_fusion), channel_id=1, source_target_pairs={{0,64},{16,80},{32,96},{48,112},{64,128},{80,144},{96,160},{112,17... | collective-permute-start | bytes 49160 | tf_op jit(solution)/shard_map/ppermute | solution.py:273
  71.7 0.4 collective-permute-start.8
  72.1 1.5 %collective-permute-done.10 = f32[2,2048]{1,0:T(2,128)S(1)} collective-permute-done((f32[2,2048]{1,0:T(2,128)S(1)}, f32[2,2048]{1,0:T(2,128)S(1)}, u32[]{:S(2)}, u32[]{:S(2)}) %collective-permute-start.10) | collective-permute-done | bytes 16416 | tf_op jit(solution)/shard_map/ppermute | solution.py:273
  73.6 1.3 %collective-permute-done.9 = f32[2,2048]{1,0:T(2,128)S(1)} collective-permute-done((f32[2,2048]{1,0:T(2,128)S(1)}, f32[2,2048]{1,0:T(2,128)S(1)}, u32[]{:S(2)}, u32[]{:S(2)}) %collective-permute-start.9) | collective-permute-done | bytes 16416 | tf_op jit(solution)/shard_map/ppermute | solution.py:273
  74.9 2.0 %collective-permute-done.8 = f32[2,2048]{1,0:T(2,128)S(1)} collective-permute-done((f32[2,2048]{1,0:T(2,128)S(1)}, f32[2,2048]{1,0:T(2,128)S(1)}, u32[]{:S(2)}, u32[]{:S(2)}) %collective-permute-start.8) | collective-permute-done | bytes 16416 | tf_op jit(solution)/shard_map/ppermute | solution.py:273
  77.0 3.8 %collective-permute-start.13 = (f32[2,2048]{1,0:T(2,128)S(1)}, f32[2,2048]{1,0:T(2,128)S(1)}, u32[]{:S(2)}, u32[]{:S(2)}) collective-permute-start(f32[2,2048]{1,0:T(2,128)S(1)} %add_add_fusion.1), channel_id=1, source_target_pairs={{0,48},{16,0},{32,16},{48,32},{64,112},{80,64},{96,80},{112,96},{1... | collective-permute-start | bytes 49160 | tf_op jit(solution)/shard_map/ppermute | solution.py:273
  80.8 0.0 collective-permute-start.12
  80.8 3.2 %collective-permute-start.11 = (f32[2,2048]{1,0:T(2,128)S(1)}, f32[2,2048]{1,0:T(2,128)S(1)}, u32[]{:S(2)}, u32[]{:S(2)}) collective-permute-start(f32[2,2048]{1,0:T(2,128)S(1)} %add_add_fusion.1), channel_id=1, source_target_pairs={{0,32},{16,48},{32,0},{48,16},{64,96},{80,112},{96,64},{112,80},{1... | collective-permute-start | bytes 49160 | tf_op jit(solution)/shard_map/ppermute | solution.py:273
  83.9 0.0 collective-permute-done.13
  83.9 2.7 %collective-permute-done.12 = f32[2,2048]{1,0:T(2,128)S(1)} collective-permute-done((f32[2,2048]{1,0:T(2,128)S(1)}, f32[2,2048]{1,0:T(2,128)S(1)}, u32[]{:S(2)}, u32[]{:S(2)}) %collective-permute-start.12) | collective-permute-done | bytes 16416 | tf_op jit(solution)/shard_map/ppermute | solution.py:273
  86.6 1.8 %collective-permute-done.11 = f32[2,2048]{1,0:T(2,128)S(1)} collective-permute-done((f32[2,2048]{1,0:T(2,128)S(1)}, f32[2,2048]{1,0:T(2,128)S(1)}, u32[]{:S(2)}, u32[]{:S(2)}) %collective-permute-start.11) | collective-permute-done | bytes 16416 | tf_op jit(solution)/shard_map/ppermute | solution.py:273
  88.4 0.6 slice_divide_fusion
  89.1 0.6 broadcast_subtract_fusion
  (7 shorter events, 0.1 us)
Async XLA Ops:
  9.4 18.0 %copy-start = (f32[32,2560]{1,0:T(8,128)S(1)}, f32[32,2560]{1,0:T(8,128)}, u32[]{:S(2)}) copy-start(f32[32,2560]{1,0:T(8,128)} %shard_map.68) | copy-start | bytes 983044
  24.5 17.2 %collective-permute-start.2 = (f32[32,2560]{1,0:T(8,128)}, f32[32,2560]{1,0:T(8,128)S(1)}, u32[]{:S(2)}, u32[]{:S(2)}) collective-permute-start(f32[32,2560]{1,0:T(8,128)} %get-tuple-element.17), channel_id=1, source_target_pairs={{0,192},{16,208},{32,224},{48,240},{64,0},{80,16},{96,32},{112,48}... | collective-permute-start | bytes 983048 | tf_op jit(solution)/shard_map/ppermute | solution.py:273
  27.4 17.6 %collective-permute-start.1 = (f32[32,2560]{1,0:T(8,128)}, f32[32,2560]{1,0:T(8,128)S(1)}, u32[]{:S(2)}, u32[]{:S(2)}) collective-permute-start(f32[32,2560]{1,0:T(8,128)} %get-tuple-element.16), channel_id=1, source_target_pairs={{0,64},{16,80},{32,96},{48,112},{64,128},{80,144},{96,160},{112,17... | collective-permute-start | bytes 983048 | tf_op jit(solution)/shard_map/ppermute | solution.py:273
  27.4 17.6 %collective-permute-start = (f32[32,2560]{1,0:T(8,128)S(1)}, f32[32,2560]{1,0:T(8,128)S(1)}, u32[]{:S(2)}, u32[]{:S(2)}) collective-permute-start(f32[32,2560]{1,0:T(8,128)S(1)} %copy-done), channel_id=1, source_target_pairs={{0,128},{16,144},{32,160},{48,176},{64,192},{80,208},{96,224},{112... | collective-permute-start | bytes 983048 | tf_op jit(solution)/shard_map/ppermute | solution.py:273
  46.1 10.2 %collective-permute-start.5 = (f32[8,2560]{1,0:T(8,128)S(1)}, f32[8,2560]{1,0:T(8,128)S(1)}, u32[]{:S(2)}, u32[]{:S(2)}) collective-permute-start(f32[8,2560]{1,0:T(8,128)S(1)} %get-tuple-element.21), channel_id=1, source_target_pairs={{0,48},{16,0},{32,16},{48,32},{64,112},{80,64},{96,80},{112,96},{1... | collective-permute-start | bytes 245768 | tf_op jit(solution)/shard_map/ppermute | solution.py:273
  52.5 6.9 %collective-permute-start.4 = (f32[8,2560]{1,0:T(8,128)S(1)}, f32[8,2560]{1,0:T(8,128)S(1)}, u32[]{:S(2)}, u32[]{:S(2)}) collective-permute-start(f32[8,2560]{1,0:T(8,128)S(1)} %get-tuple-element.22), channel_id=1, source_target_pairs={{0,16},{16,32},{32,48},{48,0},{64,80},{80,96},{96,112},{112,64},{1... | collective-permute-start | bytes 245768 | tf_op jit(solution)/shard_map/ppermute | solution.py:273
  52.5 9.2 %collective-permute-start.3 = (f32[8,2560]{1,0:T(8,128)S(1)}, f32[8,2560]{1,0:T(8,128)S(1)}, u32[]{:S(2)}, u32[]{:S(2)}) collective-permute-start(f32[8,2560]{1,0:T(8,128)S(1)} %get-tuple-element.20), channel_id=1, source_target_pairs={{0,32},{16,48},{32,0},{48,16},{64,96},{80,112},{96,64},{112,80},{1... | collective-permute-start | bytes 245768 | tf_op jit(solution)/shard_map/ppermute | solution.py:273
  61.7 4.4 %collective-permute-start.7 = (f32[8,256]{1,0:T(8,128)S(1)}, f32[8,256]{1,0:T(8,128)S(1)}, u32[]{:S(2)}, u32[]{:S(2)}) collective-permute-start(f32[8,256]{1,0:T(8,128)S(1)} %get-tuple-element.24), channel_id=1, source_target_pairs={{1,0},{2,1},{3,2},{4,3},{5,4},{6,5},{7,6},{8,7},{9,8},{10,9},{11,1... | collective-permute-start | bytes 24584 | tf_op jit(solution)/shard_map/ppermute | solution.py:308
  63.6 5.9 %collective-permute-start.6 = (f32[8,256]{1,0:T(8,128)S(1)}, f32[8,256]{1,0:T(8,128)S(1)}, u32[]{:S(2)}, u32[]{:S(2)}) collective-permute-start(f32[8,256]{1,0:T(8,128)S(1)} %get-tuple-element.23), channel_id=1, source_target_pairs={{0,1},{1,2},{2,3},{3,4},{4,5},{5,6},{6,7},{7,8},{8,9},{9,10},{10,1... | collective-permute-start | bytes 24584 | tf_op jit(solution)/shard_map/ppermute | solution.py:309
  69.6 4.0 %collective-permute-start.10 = (f32[2,2048]{1,0:T(2,128)S(1)}, f32[2,2048]{1,0:T(2,128)S(1)}, u32[]{:S(2)}, u32[]{:S(2)}) collective-permute-start(f32[2,2048]{1,0:T(2,128)S(1)} %pad_maximum_fusion), channel_id=1, source_target_pairs={{0,192},{16,208},{32,224},{48,240},{64,0},{80,16},{96,32},{112,48}... | collective-permute-start | bytes 49160 | tf_op jit(solution)/shard_map/ppermute | solution.py:273
  69.7 5.2 %collective-permute-start.9 = (f32[2,2048]{1,0:T(2,128)S(1)}, f32[2,2048]{1,0:T(2,128)S(1)}, u32[]{:S(2)}, u32[]{:S(2)}) collective-permute-start(f32[2,2048]{1,0:T(2,128)S(1)} %pad_maximum_fusion), channel_id=1, source_target_pairs={{0,64},{16,80},{32,96},{48,112},{64,128},{80,144},{96,160},{112,17... | collective-permute-start | bytes 49160 | tf_op jit(solution)/shard_map/ppermute | solution.py:273
  71.7 5.2 %collective-permute-start.8 = (f32[2,2048]{1,0:T(2,128)S(1)}, f32[2,2048]{1,0:T(2,128)S(1)}, u32[]{:S(2)}, u32[]{:S(2)}) collective-permute-start(f32[2,2048]{1,0:T(2,128)S(1)} %pad_maximum_fusion), channel_id=1, source_target_pairs={{0,128},{16,144},{32,160},{48,176},{64,192},{80,208},{96,224},{112... | collective-permute-start | bytes 49160 | tf_op jit(solution)/shard_map/ppermute | solution.py:273
  77.0 6.9 %collective-permute-start.13 = (f32[2,2048]{1,0:T(2,128)S(1)}, f32[2,2048]{1,0:T(2,128)S(1)}, u32[]{:S(2)}, u32[]{:S(2)}) collective-permute-start(f32[2,2048]{1,0:T(2,128)S(1)} %add_add_fusion.1), channel_id=1, source_target_pairs={{0,48},{16,0},{32,16},{48,32},{64,112},{80,64},{96,80},{112,96},{1... | collective-permute-start | bytes 49160 | tf_op jit(solution)/shard_map/ppermute | solution.py:273
  80.8 5.8 %collective-permute-start.12 = (f32[2,2048]{1,0:T(2,128)S(1)}, f32[2,2048]{1,0:T(2,128)S(1)}, u32[]{:S(2)}, u32[]{:S(2)}) collective-permute-start(f32[2,2048]{1,0:T(2,128)S(1)} %add_add_fusion.1), channel_id=1, source_target_pairs={{0,16},{16,32},{32,48},{48,0},{64,80},{80,96},{96,112},{112,64},{1... | collective-permute-start | bytes 49160 | tf_op jit(solution)/shard_map/ppermute | solution.py:273
  80.8 7.6 %collective-permute-start.11 = (f32[2,2048]{1,0:T(2,128)S(1)}, f32[2,2048]{1,0:T(2,128)S(1)}, u32[]{:S(2)}, u32[]{:S(2)}) collective-permute-start(f32[2,2048]{1,0:T(2,128)S(1)} %add_add_fusion.1), channel_id=1, source_target_pairs={{0,32},{16,48},{32,0},{48,16},{64,96},{80,112},{96,64},{112,80},{1... | collective-permute-start | bytes 49160 | tf_op jit(solution)/shard_map/ppermute | solution.py:273

commit v2 on v1

--- a/solution.py
+++ b/solution.py
@@ -273,19 +273,21 @@
     return lax.ppermute(value, "view", pairs)
 
 
-def scatter_stage(value, mine, outer):
+def scatter_stage(value, mine):
     parts = value.reshape(SIDE, value.shape[0] // SIDE, *value.shape[1:])
     total = lax.dynamic_index_in_dim(parts, mine, 0, False)
     for by in (2, 1, 3):
         away = lax.dynamic_index_in_dim(parts, (mine + by) % SIDE, 0, False)
-        total = total + view_shift(away, *((by, 0) if outer else (0, by)))
+        away = view_shift(away, 0, by)
+        total = total + away
     return total
 
 
 def sum_stage(value, outer):
     total = value
     for by in (2, 1, 3):
-        total = total + view_shift(value, *((by, 0) if outer else (0, by)))
+        away = view_shift(value, *((by, 0) if outer else (0, by)))
+        total = total + away
     return total
 
 
@@ -303,7 +305,7 @@
         for turn, part in zip(turns, parts):
             got[turn] = view_shift(part, turn, 0) if turn else part
     slab = got[0] + got[2] + got[1] + got[3]
-    slab = scatter_stage(slab, view % SIDE, False)
+    slab = scatter_stage(slab, view % SIDE)
     tiles = lax.axis_size("tile")
     up = lax.ppermute(slab[:, :cols], "tile", [(t + 1, t) for t in range(tiles - 1)])
     down = lax.ppermute(slab[:, cols + pixels:], "tile", [(t, t + 1) for t in range(tiles - 1)])

time: 90.1 us -> 90.1 us (level)
  no operation moved by 1% of the time
where the time goes in v2:
time: 90.1 us; the launch traced here: 89.7 us
  Pallas kernels  32.6 us (36%)
  starting transfers between devices  29.1 us (32%)
  waiting for transfers between devices  24.7 us (27%)
  other arithmetic  2.49 us (3%)
    pallas_call x3, Pallas kernels, block_filter(): pl.pallas_call(functools.partial(block_kernel, turns), out_shape=[jax.Sha...  32.6 us
    ppermute x12, starting transfers between devices, view_shift(): return lax.ppermute(value, 'view', pairs)  24.8 us
    ppermute x12, waiting for transfers between devices, view_shift(): return lax.ppermute(value, 'view', pairs)  21.3 us
    ppermute x1, waiting for transfers between devices, on_device(): lax.ppermute(slab[:, cols + pixels:], 'tile', [(t, t + 1) for t in range(...  3.43 us
    ppermute x1, starting transfers between devices, on_device(): lax.ppermute(slab[:, cols + pixels:], 'tile', [(t, t + 1) for t in range(...  2.41 us
    ppermute x1, starting transfers between devices, on_device(): lax.ppermute(slab[:, :cols], 'tile', [(t + 1, t) for t in range(tiles - 1)])  1.92 us
  transfers between devices with their start and end apart: 14, of which 10 were waited for; matrix products, arithmetic and copies ran while one was open for 0% of the time, Pallas kernels for 10%

profile of v2, /device:TPU:8, one launch (start us, length us, event | category | flops | bytes accessed | tf_op | source)
XLA Modules:
  0.0 89.7 jit_solution(2867914378686799924)
XLA Ops:
  0.6 8.7 %shard_map.68 = f32[32,2560]{1,0:T(8,128)} custom-call(s32[128]{0:T(128)} %bitcast.33, bf16[32,2048]{1,0:T(8,128)(2,1)} %ref_hbm.5, bf16[32,6144]{1,0:T(8,128)(2,1)} %bitcast.30, bf16[128,4,2048]{2,1,0:T(4,128)(2,1)} %bitcast.27, f32[3,3,3,8]{3,2,1,0:T(4,128)} %filt_hbm.5), custom_call_target="tpu_custom_call" | custom-call | flops 3000000000 | bytes 2000000 | tf_op jit(solution)/shard_map/pallas_call | solution.py:259
  9.4 0.0 copy-start
  9.4 15.2 %shard_map.69 = (f32[32,2560]{1,0:T(8,128)}, f32[32,2560]{1,0:T(8,128)}) custom-call(s32[128]{0:T(128)} %bitcast.34, bf16[32,2048]{1,0:T(8,128)(2,1)} %ref_hbm.5, bf16[32,6144]{1,0:T(8,128)(2,1)} %bitcast.31, bf16[128,4,2048]{2,1,0:T(4,128)(2,1)} %bitcast.28, f32[3,3,3,8]{3,2,1,0:T(4,128)} %filt_hbm.5), custom_call_target="tpu_custom_call" | custom-call | flops 6000000000 | bytes 2000000 | tf_op jit(solution)/shard_map/pallas_call | solution.py:259
  24.5 2.8 %collective-permute-start.2 = (f32[32,2560]{1,0:T(8,128)}, f32[32,2560]{1,0:T(8,128)S(1)}, u32[]{:S(2)}, u32[]{:S(2)}) collective-permute-start(f32[32,2560]{1,0:T(8,128)} %get-tuple-element.17), channel_id=1, source_target_pairs={{0,192},{16,208},{32,224},{48,240},{64,0},{80,16},{96,32},{112,48}... | collective-permute-start | bytes 983048 | tf_op jit(solution)/shard_map/ppermute | solution.py:273
  27.4 0.0 collective-permute-start.1
  27.4 0.0 copy-done
  27.4 2.3 %collective-permute-start = (f32[32,2560]{1,0:T(8,128)S(1)}, f32[32,2560]{1,0:T(8,128)S(1)}, u32[]{:S(2)}, u32[]{:S(2)}) collective-permute-start(f32[32,2560]{1,0:T(8,128)S(1)} %copy-done), channel_id=1, source_target_pairs={{0,128},{16,144},{32,160},{48,176},{64,192},{80,208},{96,224},{112... | collective-permute-start | bytes 983048 | tf_op jit(solution)/shard_map/ppermute | solution.py:273
  29.7 8.7 %shard_map.70 = f32[32,2560]{1,0:T(8,128)} custom-call(s32[128]{0:T(128)} %bitcast.35, bf16[32,2048]{1,0:T(8,128)(2,1)} %ref_hbm.5, bf16[32,6144]{1,0:T(8,128)(2,1)} %bitcast.32, bf16[128,4,2048]{2,1,0:T(4,128)(2,1)} %bitcast.29, f32[3,3,3,8]{3,2,1,0:T(4,128)} %filt_hbm.5), custom_call_target="tpu_custom_call" | custom-call | flops 3000000000 | bytes 2000000 | tf_op jit(solution)/shard_map/pallas_call | solution.py:259
  38.5 3.3 %collective-permute-done.2 = f32[32,2560]{1,0:T(8,128)S(1)} collective-permute-done((f32[32,2560]{1,0:T(8,128)}, f32[32,2560]{1,0:T(8,128)S(1)}, u32[]{:S(2)}, u32[]{:S(2)}) %collective-permute-start.2) | collective-permute-done | bytes 327712 | tf_op jit(solution)/shard_map/ppermute | solution.py:273
  41.7 3.3 %collective-permute-done.1 = f32[32,2560]{1,0:T(8,128)S(1)} collective-permute-done((f32[32,2560]{1,0:T(8,128)}, f32[32,2560]{1,0:T(8,128)S(1)}, u32[]{:S(2)}, u32[]{:S(2)}) %collective-permute-start.1) | collective-permute-done | bytes 327712 | tf_op jit(solution)/shard_map/ppermute | solution.py:273
  45.0 0.0 collective-permute-done
  45.0 1.0 %add_bitcast_fusion = f32[4,8,2560]{2,1,0:T(8,128)S(1)} fusion(f32[32,2560]{1,0:T(8,128)S(1)} %collective-permute-done.2, f32[32,2560]{1,0:T(8,128)S(1)} %collective-permute-done.1, f32[32,2560]{1,0:T(8,128)} %shard_map.70, f32[32,2560]{1,0:T(8,128)S(1)} %collective-permute-done), kind=kLoop, calls=%fused_computation | loop fusion | flops 245760 | bytes 1638400 | tf_op jit(solution)/shard_map/reshape | solution.py:277
  46.1 6.4 %collective-permute-start.5 = (f32[8,2560]{1,0:T(8,128)S(1)}, f32[8,2560]{1,0:T(8,128)S(1)}, u32[]{:S(2)}, u32[]{:S(2)}) collective-permute-start(f32[8,2560]{1,0:T(8,128)S(1)} %get-tuple-element.21), channel_id=1, source_target_pairs={{0,48},{16,0},{32,16},{48,32},{64,112},{80,64},{96,80},{112,96},{1... | collective-permute-start | bytes 245768 | tf_op jit(solution)/shard_map/ppermute | solution.py:273
  52.5 0.0 collective-permute-start.4
  52.5 3.8 %collective-permute-start.3 = (f32[8,2560]{1,0:T(8,128)S(1)}, f32[8,2560]{1,0:T(8,128)S(1)}, u32[]{:S(2)}, u32[]{:S(2)}) collective-permute-start(f32[8,2560]{1,0:T(8,128)S(1)} %get-tuple-element.20), channel_id=1, source_target_pairs={{0,32},{16,48},{32,0},{48,16},{64,96},{80,112},{96,64},{112,80},{1... | collective-permute-start | bytes 245768 | tf_op jit(solution)/shard_map/ppermute | solution.py:273
  56.3 0.0 collective-permute-done.5
  56.3 3.1 %collective-permute-done.4 = f32[8,2560]{1,0:T(8,128)S(1)} collective-permute-done((f32[8,2560]{1,0:T(8,128)S(1)}, f32[8,2560]{1,0:T(8,128)S(1)}, u32[]{:S(2)}, u32[]{:S(2)}) %collective-permute-start.4) | collective-permute-done | bytes 81952 | tf_op jit(solution)/shard_map/ppermute | solution.py:273
  59.4 2.2 %collective-permute-done.3 = f32[8,2560]{1,0:T(8,128)S(1)} collective-permute-done((f32[8,2560]{1,0:T(8,128)S(1)}, f32[8,2560]{1,0:T(8,128)S(1)}, u32[]{:S(2)}, u32[]{:S(2)}) %collective-permute-start.3) | collective-permute-done | bytes 81952 | tf_op jit(solution)/shard_map/ppermute | solution.py:273
  61.7 1.9 %collective-permute-start.7 = (f32[8,256]{1,0:T(8,128)S(1)}, f32[8,256]{1,0:T(8,128)S(1)}, u32[]{:S(2)}, u32[]{:S(2)}) collective-permute-start(f32[8,256]{1,0:T(8,128)S(1)} %get-tuple-element.24), channel_id=1, source_target_pairs={{1,0},{2,1},{3,2},{4,3},{5,4},{6,5},{7,6},{8,7},{9,8},{10,9},{11,1... | collective-permute-start | bytes 24584 | tf_op jit(solution)/shard_map/ppermute | solution.py:310
  63.6 2.4 %collective-permute-start.6 = (f32[8,256]{1,0:T(8,128)S(1)}, f32[8,256]{1,0:T(8,128)S(1)}, u32[]{:S(2)}, u32[]{:S(2)}) collective-permute-start(f32[8,256]{1,0:T(8,128)S(1)} %get-tuple-element.23), channel_id=1, source_target_pairs={{0,1},{1,2},{2,3},{3,4},{4,5},{5,6},{6,7},{7,8},{8,9},{9,10},{10,1... | collective-permute-start | bytes 24584 | tf_op jit(solution)/shard_map/ppermute | solution.py:311
  66.0 0.0 collective-permute-done.7
  66.1 3.4 %collective-permute-done.6 = f32[8,256]{1,0:T(8,128)S(1)} collective-permute-done((f32[8,256]{1,0:T(8,128)S(1)}, f32[8,256]{1,0:T(8,128)S(1)}, u32[]{:S(2)}, u32[]{:S(2)}) %collective-permute-start.6) | collective-permute-done | bytes 8224 | tf_op jit(solution)/shard_map/ppermute | solution.py:311
  69.5 0.1 exponential_reduce_fusion
  69.6 0.1 collective-permute-start.10
  69.7 2.0 %collective-permute-start.9 = (f32[2,2048]{1,0:T(2,128)S(1)}, f32[2,2048]{1,0:T(2,128)S(1)}, u32[]{:S(2)}, u32[]{:S(2)}) collective-permute-start(f32[2,2048]{1,0:T(2,128)S(1)} %pad_maximum_fusion), channel_id=1, source_target_pairs={{0,64},{16,80},{32,96},{48,112},{64,128},{80,144},{96,160},{112,17... | collective-permute-start | bytes 49160 | tf_op jit(solution)/shard_map/ppermute | solution.py:273
  71.7 0.4 collective-permute-start.8
  72.1 1.5 %collective-permute-done.10 = f32[2,2048]{1,0:T(2,128)S(1)} collective-permute-done((f32[2,2048]{1,0:T(2,128)S(1)}, f32[2,2048]{1,0:T(2,128)S(1)}, u32[]{:S(2)}, u32[]{:S(2)}) %collective-permute-start.10) | collective-permute-done | bytes 16416 | tf_op jit(solution)/shard_map/ppermute | solution.py:273
  73.6 1.3 %collective-permute-done.9 = f32[2,2048]{1,0:T(2,128)S(1)} collective-permute-done((f32[2,2048]{1,0:T(2,128)S(1)}, f32[2,2048]{1,0:T(2,128)S(1)}, u32[]{:S(2)}, u32[]{:S(2)}) %collective-permute-start.9) | collective-permute-done | bytes 16416 | tf_op jit(solution)/shard_map/ppermute | solution.py:273
  74.9 2.0 %collective-permute-done.8 = f32[2,2048]{1,0:T(2,128)S(1)} collective-permute-done((f32[2,2048]{1,0:T(2,128)S(1)}, f32[2,2048]{1,0:T(2,128)S(1)}, u32[]{:S(2)}, u32[]{:S(2)}) %collective-permute-start.8) | collective-permute-done | bytes 16416 | tf_op jit(solution)/shard_map/ppermute | solution.py:273
  77.0 3.8 %collective-permute-start.13 = (f32[2,2048]{1,0:T(2,128)S(1)}, f32[2,2048]{1,0:T(2,128)S(1)}, u32[]{:S(2)}, u32[]{:S(2)}) collective-permute-start(f32[2,2048]{1,0:T(2,128)S(1)} %add_add_fusion.1), channel_id=1, source_target_pairs={{0,48},{16,0},{32,16},{48,32},{64,112},{80,64},{96,80},{112,96},{1... | collective-permute-start | bytes 49160 | tf_op jit(solution)/shard_map/ppermute | solution.py:273
  80.8 0.0 collective-permute-start.12
  80.8 3.2 %collective-permute-start.11 = (f32[2,2048]{1,0:T(2,128)S(1)}, f32[2,2048]{1,0:T(2,128)S(1)}, u32[]{:S(2)}, u32[]{:S(2)}) collective-permute-start(f32[2,2048]{1,0:T(2,128)S(1)} %add_add_fusion.1), channel_id=1, source_target_pairs={{0,32},{16,48},{32,0},{48,16},{64,96},{80,112},{96,64},{112,80},{1... | collective-permute-start | bytes 49160 | tf_op jit(solution)/shard_map/ppermute | solution.py:273
  83.9 0.0 collective-permute-done.13
  83.9 2.7 %collective-permute-done.12 = f32[2,2048]{1,0:T(2,128)S(1)} collective-permute-done((f32[2,2048]{1,0:T(2,128)S(1)}, f32[2,2048]{1,0:T(2,128)S(1)}, u32[]{:S(2)}, u32[]{:S(2)}) %collective-permute-start.12) | collective-permute-done | bytes 16416 | tf_op jit(solution)/shard_map/ppermute | solution.py:273
  86.6 1.8 %collective-permute-done.11 = f32[2,2048]{1,0:T(2,128)S(1)} collective-permute-done((f32[2,2048]{1,0:T(2,128)S(1)}, f32[2,2048]{1,0:T(2,128)S(1)}, u32[]{:S(2)}, u32[]{:S(2)}) %collective-permute-start.11) | collective-permute-done | bytes 16416 | tf_op jit(solution)/shard_map/ppermute | solution.py:273
  88.4 0.6 slice_divide_fusion
  89.1 0.6 broadcast_subtract_fusion
  (7 shorter events, 0.1 us)
Async XLA Ops:
  9.4 18.0 %copy-start = (f32[32,2560]{1,0:T(8,128)S(1)}, f32[32,2560]{1,0:T(8,128)}, u32[]{:S(2)}) copy-start(f32[32,2560]{1,0:T(8,128)} %shard_map.68) | copy-start | bytes 983044
  24.5 17.2 %collective-permute-start.2 = (f32[32,2560]{1,0:T(8,128)}, f32[32,2560]{1,0:T(8,128)S(1)}, u32[]{:S(2)}, u32[]{:S(2)}) collective-permute-start(f32[32,2560]{1,0:T(8,128)} %get-tuple-element.17), channel_id=1, source_target_pairs={{0,192},{16,208},{32,224},{48,240},{64,0},{80,16},{96,32},{112,48}... | collective-permute-start | bytes 983048 | tf_op jit(solution)/shard_map/ppermute | solution.py:273
  27.4 17.6 %collective-permute-start.1 = (f32[32,2560]{1,0:T(8,128)}, f32[32,2560]{1,0:T(8,128)S(1)}, u32[]{:S(2)}, u32[]{:S(2)}) collective-permute-start(f32[32,2560]{1,0:T(8,128)} %get-tuple-element.16), channel_id=1, source_target_pairs={{0,64},{16,80},{32,96},{48,112},{64,128},{80,144},{96,160},{112,17... | collective-permute-start | bytes 983048 | tf_op jit(solution)/shard_map/ppermute | solution.py:273
  27.4 17.6 %collective-permute-start = (f32[32,2560]{1,0:T(8,128)S(1)}, f32[32,2560]{1,0:T(8,128)S(1)}, u32[]{:S(2)}, u32[]{:S(2)}) collective-permute-start(f32[32,2560]{1,0:T(8,128)S(1)} %copy-done), channel_id=1, source_target_pairs={{0,128},{16,144},{32,160},{48,176},{64,192},{80,208},{96,224},{112... | collective-permute-start | bytes 983048 | tf_op jit(solution)/shard_map/ppermute | solution.py:273
  46.1 10.2 %collective-permute-start.5 = (f32[8,2560]{1,0:T(8,128)S(1)}, f32[8,2560]{1,0:T(8,128)S(1)}, u32[]{:S(2)}, u32[]{:S(2)}) collective-permute-start(f32[8,2560]{1,0:T(8,128)S(1)} %get-tuple-element.21), channel_id=1, source_target_pairs={{0,48},{16,0},{32,16},{48,32},{64,112},{80,64},{96,80},{112,96},{1... | collective-permute-start | bytes 245768 | tf_op jit(solution)/shard_map/ppermute | solution.py:273
  52.5 6.9 %collective-permute-start.4 = (f32[8,2560]{1,0:T(8,128)S(1)}, f32[8,2560]{1,0:T(8,128)S(1)}, u32[]{:S(2)}, u32[]{:S(2)}) collective-permute-start(f32[8,2560]{1,0:T(8,128)S(1)} %get-tuple-element.22), channel_id=1, source_target_pairs={{0,16},{16,32},{32,48},{48,0},{64,80},{80,96},{96,112},{112,64},{1... | collective-permute-start | bytes 245768 | tf_op jit(solution)/shard_map/ppermute | solution.py:273
  52.5 9.2 %collective-permute-start.3 = (f32[8,2560]{1,0:T(8,128)S(1)}, f32[8,2560]{1,0:T(8,128)S(1)}, u32[]{:S(2)}, u32[]{:S(2)}) collective-permute-start(f32[8,2560]{1,0:T(8,128)S(1)} %get-tuple-element.20), channel_id=1, source_target_pairs={{0,32},{16,48},{32,0},{48,16},{64,96},{80,112},{96,64},{112,80},{1... | collective-permute-start | bytes 245768 | tf_op jit(solution)/shard_map/ppermute | solution.py:273
  61.7 4.4 %collective-permute-start.7 = (f32[8,256]{1,0:T(8,128)S(1)}, f32[8,256]{1,0:T(8,128)S(1)}, u32[]{:S(2)}, u32[]{:S(2)}) collective-permute-start(f32[8,256]{1,0:T(8,128)S(1)} %get-tuple-element.24), channel_id=1, source_target_pairs={{1,0},{2,1},{3,2},{4,3},{5,4},{6,5},{7,6},{8,7},{9,8},{10,9},{11,1... | collective-permute-start | bytes 24584 | tf_op jit(solution)/shard_map/ppermute | solution.py:310
  63.6 5.9 %collective-permute-start.6 = (f32[8,256]{1,0:T(8,128)S(1)}, f32[8,256]{1,0:T(8,128)S(1)}, u32[]{:S(2)}, u32[]{:S(2)}) collective-permute-start(f32[8,256]{1,0:T(8,128)S(1)} %get-tuple-element.23), channel_id=1, source_target_pairs={{0,1},{1,2},{2,3},{3,4},{4,5},{5,6},{6,7},{7,8},{8,9},{9,10},{10,1... | collective-permute-start | bytes 24584 | tf_op jit(solution)/shard_map/ppermute | solution.py:311
  69.6 4.0 %collective-permute-start.10 = (f32[2,2048]{1,0:T(2,128)S(1)}, f32[2,2048]{1,0:T(2,128)S(1)}, u32[]{:S(2)}, u32[]{:S(2)}) collective-permute-start(f32[2,2048]{1,0:T(2,128)S(1)} %pad_maximum_fusion), channel_id=1, source_target_pairs={{0,192},{16,208},{32,224},{48,240},{64,0},{80,16},{96,32},{112,48}... | collective-permute-start | bytes 49160 | tf_op jit(solution)/shard_map/ppermute | solution.py:273
  69.7 5.2 %collective-permute-start.9 = (f32[2,2048]{1,0:T(2,128)S(1)}, f32[2,2048]{1,0:T(2,128)S(1)}, u32[]{:S(2)}, u32[]{:S(2)}) collective-permute-start(f32[2,2048]{1,0:T(2,128)S(1)} %pad_maximum_fusion), channel_id=1, source_target_pairs={{0,64},{16,80},{32,96},{48,112},{64,128},{80,144},{96,160},{112,17... | collective-permute-start | bytes 49160 | tf_op jit(solution)/shard_map/ppermute | solution.py:273
  71.7 5.2 %collective-permute-start.8 = (f32[2,2048]{1,0:T(2,128)S(1)}, f32[2,2048]{1,0:T(2,128)S(1)}, u32[]{:S(2)}, u32[]{:S(2)}) collective-permute-start(f32[2,2048]{1,0:T(2,128)S(1)} %pad_maximum_fusion), channel_id=1, source_target_pairs={{0,128},{16,144},{32,160},{48,176},{64,192},{80,208},{96,224},{112... | collective-permute-start | bytes 49160 | tf_op jit(solution)/shard_map/ppermute | solution.py:273
  77.0 6.9 %collective-permute-start.13 = (f32[2,2048]{1,0:T(2,128)S(1)}, f32[2,2048]{1,0:T(2,128)S(1)}, u32[]{:S(2)}, u32[]{:S(2)}) collective-permute-start(f32[2,2048]{1,0:T(2,128)S(1)} %add_add_fusion.1), channel_id=1, source_target_pairs={{0,48},{16,0},{32,16},{48,32},{64,112},{80,64},{96,80},{112,96},{1... | collective-permute-start | bytes 49160 | tf_op jit(solution)/shard_map/ppermute | solution.py:273
  80.8 5.8 %collective-permute-start.12 = (f32[2,2048]{1,0:T(2,128)S(1)}, f32[2,2048]{1,0:T(2,128)S(1)}, u32[]{:S(2)}, u32[]{:S(2)}) collective-permute-start(f32[2,2048]{1,0:T(2,128)S(1)} %add_add_fusion.1), channel_id=1, source_target_pairs={{0,16},{16,32},{32,48},{48,0},{64,80},{80,96},{96,112},{112,64},{1... | collective-permute-start | bytes 49160 | tf_op jit(solution)/shard_map/ppermute | solution.py:273
  80.8 7.6 %collective-permute-start.11 = (f32[2,2048]{1,0:T(2,128)S(1)}, f32[2,2048]{1,0:T(2,128)S(1)}, u32[]{:S(2)}, u32[]{:S(2)}) collective-permute-start(f32[2,2048]{1,0:T(2,128)S(1)} %add_add_fusion.1), channel_id=1, source_target_pairs={{0,32},{16,48},{32,0},{48,16},{64,96},{80,112},{96,64},{112,80},{1... | collective-permute-start | bytes 49160 | tf_op jit(solution)/shard_map/ppermute | solution.py:273

commit v3 on v2

--- a/solution.py
+++ b/solution.py
@@ -24,7 +24,8 @@
 
 def block_kernel(turns, taps_ref, ref_hbm, src_hbm, w_hbm, filt_hbm, *refs):
     outs, refs = refs[:len(turns)], refs[len(turns):]
-    (ref_ref, src_ref, filt_ref, win, base, tmp, wbuf, wf, high, low, lhs, slide, out_ref, sem) = refs
+    (ref_ref, src_ref, filt_ref, win, base, tmp, wbuf, wf, high, low, lhs, slide, held_out, sem) = refs
+    out_ref = outs[0] if len(turns) == 1 else held_out
     depth = w_hbm.shape[0]
     count = out_ref.shape[0]
     step = pl.program_id(0)
@@ -217,7 +218,7 @@
         low[end - G:end, :] = jnp.zeros((G, high.shape[1]), jnp.bfloat16)
 
     filter_group(groups - 1)
-    for n in range(len(turns)):
+    for n in range(len(turns) if len(turns) > 1 else 0):
         @pl.when(step == n)
         def _():
             outs[n][...] = out_ref[...]

time: 90.1 us -> 90.1 us (level)
  no operation moved by 1% of the time
where the time goes in v3:
time: 90.1 us; the launch traced here: 89.7 us
  Pallas kernels  32.6 us (36%)
  starting transfers between devices  29.1 us (32%)
  waiting for transfers between devices  24.7 us (27%)
  other arithmetic  2.49 us (3%)
    pallas_call x3, Pallas kernels, block_filter(): pl.pallas_call(functools.partial(block_kernel, turns), out_shape=[jax.Sha...  32.6 us
    ppermute x12, starting transfers between devices, view_shift(): return lax.ppermute(value, 'view', pairs)  24.8 us
    ppermute x12, waiting for transfers between devices, view_shift(): return lax.ppermute(value, 'view', pairs)  21.3 us
    ppermute x1, waiting for transfers between devices, on_device(): lax.ppermute(slab[:, cols + pixels:], 'tile', [(t, t + 1) for t in range(...  3.43 us
    ppermute x1, starting transfers between devices, on_device(): lax.ppermute(slab[:, cols + pixels:], 'tile', [(t, t + 1) for t in range(...  2.41 us
    ppermute x1, starting transfers between devices, on_device(): lax.ppermute(slab[:, :cols], 'tile', [(t + 1, t) for t in range(tiles - 1)])  1.92 us
  transfers between devices with their start and end apart: 14, of which 10 were waited for; matrix products, arithmetic and copies ran while one was open for 0% of the time, Pallas kernels for 10%

profile of v3, /device:TPU:8, one launch (start us, length us, event | category | flops | bytes accessed | tf_op | source)
XLA Modules:
  0.0 89.7 jit_solution(6001620330483737130)
XLA Ops:
  0.6 8.7 %shard_map.68 = f32[32,2560]{1,0:T(8,128)} custom-call(s32[128]{0:T(128)} %bitcast.33, bf16[32,2048]{1,0:T(8,128)(2,1)} %ref_hbm.5, bf16[32,6144]{1,0:T(8,128)(2,1)} %bitcast.30, bf16[128,4,2048]{2,1,0:T(4,128)(2,1)} %bitcast.27, f32[3,3,3,8]{3,2,1,0:T(4,128)} %filt_hbm.5), custom_call_target="tpu_custom_call" | custom-call | flops 3000000000 | bytes 2000000 | tf_op jit(solution)/shard_map/pallas_call | solution.py:260
  9.4 0.0 copy-start
  9.4 15.2 %shard_map.69 = (f32[32,2560]{1,0:T(8,128)}, f32[32,2560]{1,0:T(8,128)}) custom-call(s32[128]{0:T(128)} %bitcast.34, bf16[32,2048]{1,0:T(8,128)(2,1)} %ref_hbm.5, bf16[32,6144]{1,0:T(8,128)(2,1)} %bitcast.31, bf16[128,4,2048]{2,1,0:T(4,128)(2,1)} %bitcast.28, f32[3,3,3,8]{3,2,1,0:T(4,128)} %filt_hbm.5), custom_call_target="tpu_custom_call" | custom-call | flops 6000000000 | bytes 2000000 | tf_op jit(solution)/shard_map/pallas_call | solution.py:260
  24.5 2.8 %collective-permute-start.2 = (f32[32,2560]{1,0:T(8,128)}, f32[32,2560]{1,0:T(8,128)S(1)}, u32[]{:S(2)}, u32[]{:S(2)}) collective-permute-start(f32[32,2560]{1,0:T(8,128)} %get-tuple-element.17), channel_id=1, source_target_pairs={{0,192},{16,208},{32,224},{48,240},{64,0},{80,16},{96,32},{112,48}... | collective-permute-start | bytes 983048 | tf_op jit(solution)/shard_map/ppermute | solution.py:274
  27.4 0.0 collective-permute-start.1
  27.4 0.0 copy-done
  27.4 2.3 %collective-permute-start = (f32[32,2560]{1,0:T(8,128)S(1)}, f32[32,2560]{1,0:T(8,128)S(1)}, u32[]{:S(2)}, u32[]{:S(2)}) collective-permute-start(f32[32,2560]{1,0:T(8,128)S(1)} %copy-done), channel_id=1, source_target_pairs={{0,128},{16,144},{32,160},{48,176},{64,192},{80,208},{96,224},{112... | collective-permute-start | bytes 983048 | tf_op jit(solution)/shard_map/ppermute | solution.py:274
  29.7 8.7 %shard_map.70 = f32[32,2560]{1,0:T(8,128)} custom-call(s32[128]{0:T(128)} %bitcast.35, bf16[32,2048]{1,0:T(8,128)(2,1)} %ref_hbm.5, bf16[32,6144]{1,0:T(8,128)(2,1)} %bitcast.32, bf16[128,4,2048]{2,1,0:T(4,128)(2,1)} %bitcast.29, f32[3,3,3,8]{3,2,1,0:T(4,128)} %filt_hbm.5), custom_call_target="tpu_custom_call" | custom-call | flops 3000000000 | bytes 2000000 | tf_op jit(solution)/shard_map/pallas_call | solution.py:260
  38.5 3.3 %collective-permute-done.2 = f32[32,2560]{1,0:T(8,128)S(1)} collective-permute-done((f32[32,2560]{1,0:T(8,128)}, f32[32,2560]{1,0:T(8,128)S(1)}, u32[]{:S(2)}, u32[]{:S(2)}) %collective-permute-start.2) | collective-permute-done | bytes 327712 | tf_op jit(solution)/shard_map/ppermute | solution.py:274
  41.7 3.3 %collective-permute-done.1 = f32[32,2560]{1,0:T(8,128)S(1)} collective-permute-done((f32[32,2560]{1,0:T(8,128)}, f32[32,2560]{1,0:T(8,128)S(1)}, u32[]{:S(2)}, u32[]{:S(2)}) %collective-permute-start.1) | collective-permute-done | bytes 327712 | tf_op jit(solution)/shard_map/ppermute | solution.py:274
  45.0 0.0 collective-permute-done
  45.0 1.0 %add_bitcast_fusion = f32[4,8,2560]{2,1,0:T(8,128)S(1)} fusion(f32[32,2560]{1,0:T(8,128)S(1)} %collective-permute-done.2, f32[32,2560]{1,0:T(8,128)S(1)} %collective-permute-done.1, f32[32,2560]{1,0:T(8,128)} %shard_map.70, f32[32,2560]{1,0:T(8,128)S(1)} %collective-permute-done), kind=kLoop, calls=%fused_computation | loop fusion | flops 245760 | bytes 1638400 | tf_op jit(solution)/shard_map/reshape | solution.py:278
  46.1 6.4 %collective-permute-start.5 = (f32[8,2560]{1,0:T(8,128)S(1)}, f32[8,2560]{1,0:T(8,128)S(1)}, u32[]{:S(2)}, u32[]{:S(2)}) collective-permute-start(f32[8,2560]{1,0:T(8,128)S(1)} %get-tuple-element.21), channel_id=1, source_target_pairs={{0,48},{16,0},{32,16},{48,32},{64,112},{80,64},{96,80},{112,96},{1... | collective-permute-start | bytes 245768 | tf_op jit(solution)/shard_map/ppermute | solution.py:274
  52.5 0.0 collective-permute-start.4
  52.5 3.8 %collective-permute-start.3 = (f32[8,2560]{1,0:T(8,128)S(1)}, f32[8,2560]{1,0:T(8,128)S(1)}, u32[]{:S(2)}, u32[]{:S(2)}) collective-permute-start(f32[8,2560]{1,0:T(8,128)S(1)} %get-tuple-element.20), channel_id=1, source_target_pairs={{0,32},{16,48},{32,0},{48,16},{64,96},{80,112},{96,64},{112,80},{1... | collective-permute-start | bytes 245768 | tf_op jit(solution)/shard_map/ppermute | solution.py:274
  56.3 0.0 collective-permute-done.5
  56.3 3.1 %collective-permute-done.4 = f32[8,2560]{1,0:T(8,128)S(1)} collective-permute-done((f32[8,2560]{1,0:T(8,128)S(1)}, f32[8,2560]{1,0:T(8,128)S(1)}, u32[]{:S(2)}, u32[]{:S(2)}) %collective-permute-start.4) | collective-permute-done | bytes 81952 | tf_op jit(solution)/shard_map/ppermute | solution.py:274
  59.4 2.2 %collective-permute-done.3 = f32[8,2560]{1,0:T(8,128)S(1)} collective-permute-done((f32[8,2560]{1,0:T(8,128)S(1)}, f32[8,2560]{1,0:T(8,128)S(1)}, u32[]{:S(2)}, u32[]{:S(2)}) %collective-permute-start.3) | collective-permute-done | bytes 81952 | tf_op jit(solution)/shard_map/ppermute | solution.py:274
  61.7 1.9 %collective-permute-start.7 = (f32[8,256]{1,0:T(8,128)S(1)}, f32[8,256]{1,0:T(8,128)S(1)}, u32[]{:S(2)}, u32[]{:S(2)}) collective-permute-start(f32[8,256]{1,0:T(8,128)S(1)} %get-tuple-element.24), channel_id=1, source_target_pairs={{1,0},{2,1},{3,2},{4,3},{5,4},{6,5},{7,6},{8,7},{9,8},{10,9},{11,1... | collective-permute-start | bytes 24584 | tf_op jit(solution)/shard_map/ppermute | solution.py:311
  63.6 2.4 %collective-permute-start.6 = (f32[8,256]{1,0:T(8,128)S(1)}, f32[8,256]{1,0:T(8,128)S(1)}, u32[]{:S(2)}, u32[]{:S(2)}) collective-permute-start(f32[8,256]{1,0:T(8,128)S(1)} %get-tuple-element.23), channel_id=1, source_target_pairs={{0,1},{1,2},{2,3},{3,4},{4,5},{5,6},{6,7},{7,8},{8,9},{9,10},{10,1... | collective-permute-start | bytes 24584 | tf_op jit(solution)/shard_map/ppermute | solution.py:312
  66.0 0.0 collective-permute-done.7
  66.1 3.4 %collective-permute-done.6 = f32[8,256]{1,0:T(8,128)S(1)} collective-permute-done((f32[8,256]{1,0:T(8,128)S(1)}, f32[8,256]{1,0:T(8,128)S(1)}, u32[]{:S(2)}, u32[]{:S(2)}) %collective-permute-start.6) | collective-permute-done | bytes 8224 | tf_op jit(solution)/shard_map/ppermute | solution.py:312
  69.5 0.1 exponential_reduce_fusion
  69.6 0.1 collective-permute-start.10
  69.7 2.0 %collective-permute-start.9 = (f32[2,2048]{1,0:T(2,128)S(1)}, f32[2,2048]{1,0:T(2,128)S(1)}, u32[]{:S(2)}, u32[]{:S(2)}) collective-permute-start(f32[2,2048]{1,0:T(2,128)S(1)} %pad_maximum_fusion), channel_id=1, source_target_pairs={{0,64},{16,80},{32,96},{48,112},{64,128},{80,144},{96,160},{112,17... | collective-permute-start | bytes 49160 | tf_op jit(solution)/shard_map/ppermute | solution.py:274
  71.7 0.4 collective-permute-start.8
  72.1 1.5 %collective-permute-done.10 = f32[2,2048]{1,0:T(2,128)S(1)} collective-permute-done((f32[2,2048]{1,0:T(2,128)S(1)}, f32[2,2048]{1,0:T(2,128)S(1)}, u32[]{:S(2)}, u32[]{:S(2)}) %collective-permute-start.10) | collective-permute-done | bytes 16416 | tf_op jit(solution)/shard_map/ppermute | solution.py:274
  73.6 1.3 %collective-permute-done.9 = f32[2,2048]{1,0:T(2,128)S(1)} collective-permute-done((f32[2,2048]{1,0:T(2,128)S(1)}, f32[2,2048]{1,0:T(2,128)S(1)}, u32[]{:S(2)}, u32[]{:S(2)}) %collective-permute-start.9) | collective-permute-done | bytes 16416 | tf_op jit(solution)/shard_map/ppermute | solution.py:274
  74.9 2.0 %collective-permute-done.8 = f32[2,2048]{1,0:T(2,128)S(1)} collective-permute-done((f32[2,2048]{1,0:T(2,128)S(1)}, f32[2,2048]{1,0:T(2,128)S(1)}, u32[]{:S(2)}, u32[]{:S(2)}) %collective-permute-start.8) | collective-permute-done | bytes 16416 | tf_op jit(solution)/shard_map/ppermute | solution.py:274
  77.0 3.8 %collective-permute-start.13 = (f32[2,2048]{1,0:T(2,128)S(1)}, f32[2,2048]{1,0:T(2,128)S(1)}, u32[]{:S(2)}, u32[]{:S(2)}) collective-permute-start(f32[2,2048]{1,0:T(2,128)S(1)} %add_add_fusion.1), channel_id=1, source_target_pairs={{0,48},{16,0},{32,16},{48,32},{64,112},{80,64},{96,80},{112,96},{1... | collective-permute-start | bytes 49160 | tf_op jit(solution)/shard_map/ppermute | solution.py:274
  80.8 0.0 collective-permute-start.12
  80.8 3.2 %collective-permute-start.11 = (f32[2,2048]{1,0:T(2,128)S(1)}, f32[2,2048]{1,0:T(2,128)S(1)}, u32[]{:S(2)}, u32[]{:S(2)}) collective-permute-start(f32[2,2048]{1,0:T(2,128)S(1)} %add_add_fusion.1), channel_id=1, source_target_pairs={{0,32},{16,48},{32,0},{48,16},{64,96},{80,112},{96,64},{112,80},{1... | collective-permute-start | bytes 49160 | tf_op jit(solution)/shard_map/ppermute | solution.py:274
  83.9 0.0 collective-permute-done.13
  83.9 2.7 %collective-permute-done.12 = f32[2,2048]{1,0:T(2,128)S(1)} collective-permute-done((f32[2,2048]{1,0:T(2,128)S(1)}, f32[2,2048]{1,0:T(2,128)S(1)}, u32[]{:S(2)}, u32[]{:S(2)}) %collective-permute-start.12) | collective-permute-done | bytes 16416 | tf_op jit(solution)/shard_map/ppermute | solution.py:274
  86.6 1.8 %collective-permute-done.11 = f32[2,2048]{1,0:T(2,128)S(1)} collective-permute-done((f32[2,2048]{1,0:T(2,128)S(1)}, f32[2,2048]{1,0:T(2,128)S(1)}, u32[]{:S(2)}, u32[]{:S(2)}) %collective-permute-start.11) | collective-permute-done | bytes 16416 | tf_op jit(solution)/shard_map/ppermute | solution.py:274
  88.4 0.6 slice_divide_fusion
  89.1 0.6 broadcast_subtract_fusion
  (7 shorter events, 0.1 us)
Async XLA Ops:
  9.4 18.0 %copy-start = (f32[32,2560]{1,0:T(8,128)S(1)}, f32[32,2560]{1,0:T(8,128)}, u32[]{:S(2)}) copy-start(f32[32,2560]{1,0:T(8,128)} %shard_map.68) | copy-start | bytes 983044
  24.5 17.2 %collective-permute-start.2 = (f32[32,2560]{1,0:T(8,128)}, f32[32,2560]{1,0:T(8,128)S(1)}, u32[]{:S(2)}, u32[]{:S(2)}) collective-permute-start(f32[32,2560]{1,0:T(8,128)} %get-tuple-element.17), channel_id=1, source_target_pairs={{0,192},{16,208},{32,224},{48,240},{64,0},{80,16},{96,32},{112,48}... | collective-permute-start | bytes 983048 | tf_op jit(solution)/shard_map/ppermute | solution.py:274
  27.4 17.6 %collective-permute-start.1 = (f32[32,2560]{1,0:T(8,128)}, f32[32,2560]{1,0:T(8,128)S(1)}, u32[]{:S(2)}, u32[]{:S(2)}) collective-permute-start(f32[32,2560]{1,0:T(8,128)} %get-tuple-element.16), channel_id=1, source_target_pairs={{0,64},{16,80},{32,96},{48,112},{64,128},{80,144},{96,160},{112,17... | collective-permute-start | bytes 983048 | tf_op jit(solution)/shard_map/ppermute | solution.py:274
  27.4 17.6 %collective-permute-start = (f32[32,2560]{1,0:T(8,128)S(1)}, f32[32,2560]{1,0:T(8,128)S(1)}, u32[]{:S(2)}, u32[]{:S(2)}) collective-permute-start(f32[32,2560]{1,0:T(8,128)S(1)} %copy-done), channel_id=1, source_target_pairs={{0,128},{16,144},{32,160},{48,176},{64,192},{80,208},{96,224},{112... | collective-permute-start | bytes 983048 | tf_op jit(solution)/shard_map/ppermute | solution.py:274
  46.1 10.2 %collective-permute-start.5 = (f32[8,2560]{1,0:T(8,128)S(1)}, f32[8,2560]{1,0:T(8,128)S(1)}, u32[]{:S(2)}, u32[]{:S(2)}) collective-permute-start(f32[8,2560]{1,0:T(8,128)S(1)} %get-tuple-element.21), channel_id=1, source_target_pairs={{0,48},{16,0},{32,16},{48,32},{64,112},{80,64},{96,80},{112,96},{1... | collective-permute-start | bytes 245768 | tf_op jit(solution)/shard_map/ppermute | solution.py:274
  52.5 6.9 %collective-permute-start.4 = (f32[8,2560]{1,0:T(8,128)S(1)}, f32[8,2560]{1,0:T(8,128)S(1)}, u32[]{:S(2)}, u32[]{:S(2)}) collective-permute-start(f32[8,2560]{1,0:T(8,128)S(1)} %get-tuple-element.22), channel_id=1, source_target_pairs={{0,16},{16,32},{32,48},{48,0},{64,80},{80,96},{96,112},{112,64},{1... | collective-permute-start | bytes 245768 | tf_op jit(solution)/shard_map/ppermute | solution.py:274
  52.5 9.2 %collective-permute-start.3 = (f32[8,2560]{1,0:T(8,128)S(1)}, f32[8,2560]{1,0:T(8,128)S(1)}, u32[]{:S(2)}, u32[]{:S(2)}) collective-permute-start(f32[8,2560]{1,0:T(8,128)S(1)} %get-tuple-element.20), channel_id=1, source_target_pairs={{0,32},{16,48},{32,0},{48,16},{64,96},{80,112},{96,64},{112,80},{1... | collective-permute-start | bytes 245768 | tf_op jit(solution)/shard_map/ppermute | solution.py:274
  61.7 4.4 %collective-permute-start.7 = (f32[8,256]{1,0:T(8,128)S(1)}, f32[8,256]{1,0:T(8,128)S(1)}, u32[]{:S(2)}, u32[]{:S(2)}) collective-permute-start(f32[8,256]{1,0:T(8,128)S(1)} %get-tuple-element.24), channel_id=1, source_target_pairs={{1,0},{2,1},{3,2},{4,3},{5,4},{6,5},{7,6},{8,7},{9,8},{10,9},{11,1... | collective-permute-start | bytes 24584 | tf_op jit(solution)/shard_map/ppermute | solution.py:311
  63.6 5.9 %collective-permute-start.6 = (f32[8,256]{1,0:T(8,128)S(1)}, f32[8,256]{1,0:T(8,128)S(1)}, u32[]{:S(2)}, u32[]{:S(2)}) collective-permute-start(f32[8,256]{1,0:T(8,128)S(1)} %get-tuple-element.23), channel_id=1, source_target_pairs={{0,1},{1,2},{2,3},{3,4},{4,5},{5,6},{6,7},{7,8},{8,9},{9,10},{10,1... | collective-permute-start | bytes 24584 | tf_op jit(solution)/shard_map/ppermute | solution.py:312
  69.6 4.0 %collective-permute-start.10 = (f32[2,2048]{1,0:T(2,128)S(1)}, f32[2,2048]{1,0:T(2,128)S(1)}, u32[]{:S(2)}, u32[]{:S(2)}) collective-permute-start(f32[2,2048]{1,0:T(2,128)S(1)} %pad_maximum_fusion), channel_id=1, source_target_pairs={{0,192},{16,208},{32,224},{48,240},{64,0},{80,16},{96,32},{112,48}... | collective-permute-start | bytes 49160 | tf_op jit(solution)/shard_map/ppermute | solution.py:274
  69.7 5.2 %collective-permute-start.9 = (f32[2,2048]{1,0:T(2,128)S(1)}, f32[2,2048]{1,0:T(2,128)S(1)}, u32[]{:S(2)}, u32[]{:S(2)}) collective-permute-start(f32[2,2048]{1,0:T(2,128)S(1)} %pad_maximum_fusion), channel_id=1, source_target_pairs={{0,64},{16,80},{32,96},{48,112},{64,128},{80,144},{96,160},{112,17... | collective-permute-start | bytes 49160 | tf_op jit(solution)/shard_map/ppermute | solution.py:274
  71.7 5.2 %collective-permute-start.8 = (f32[2,2048]{1,0:T(2,128)S(1)}, f32[2,2048]{1,0:T(2,128)S(1)}, u32[]{:S(2)}, u32[]{:S(2)}) collective-permute-start(f32[2,2048]{1,0:T(2,128)S(1)} %pad_maximum_fusion), channel_id=1, source_target_pairs={{0,128},{16,144},{32,160},{48,176},{64,192},{80,208},{96,224},{112... | collective-permute-start | bytes 49160 | tf_op jit(solution)/shard_map/ppermute | solution.py:274
  77.0 6.9 %collective-permute-start.13 = (f32[2,2048]{1,0:T(2,128)S(1)}, f32[2,2048]{1,0:T(2,128)S(1)}, u32[]{:S(2)}, u32[]{:S(2)}) collective-permute-start(f32[2,2048]{1,0:T(2,128)S(1)} %add_add_fusion.1), channel_id=1, source_target_pairs={{0,48},{16,0},{32,16},{48,32},{64,112},{80,64},{96,80},{112,96},{1... | collective-permute-start | bytes 49160 | tf_op jit(solution)/shard_map/ppermute | solution.py:274
  80.8 5.8 %collective-permute-start.12 = (f32[2,2048]{1,0:T(2,128)S(1)}, f32[2,2048]{1,0:T(2,128)S(1)}, u32[]{:S(2)}, u32[]{:S(2)}) collective-permute-start(f32[2,2048]{1,0:T(2,128)S(1)} %add_add_fusion.1), channel_id=1, source_target_pairs={{0,16},{16,32},{32,48},{48,0},{64,80},{80,96},{96,112},{112,64},{1... | collective-permute-start | bytes 49160 | tf_op jit(solution)/shard_map/ppermute | solution.py:274
  80.8 7.6 %collective-permute-start.11 = (f32[2,2048]{1,0:T(2,128)S(1)}, f32[2,2048]{1,0:T(2,128)S(1)}, u32[]{:S(2)}, u32[]{:S(2)}) collective-permute-start(f32[2,2048]{1,0:T(2,128)S(1)} %add_add_fusion.1), channel_id=1, source_target_pairs={{0,32},{16,48},{32,0},{48,16},{64,96},{80,112},{96,64},{112,80},{1... | collective-permute-start | bytes 49160 | tf_op jit(solution)/shard_map/ppermute | solution.py:274
